TPU v7x, 256 devices: a whole 4x4x8 slice. The times are simulated.
256 devices in a mesh: row: 16 (over z, core), col: 16 (over x, y).
Axes of the slice: x: 4, y: 4, z: 8, core: 2. Of those that a mesh axis runs over, the one named last changes fastest.
Arguments:
- tensor: float32 [12, 8192, 8192], P(None, 'row', 'col'), may hold values from -6 to 6
- factor_b: float32 [8192, 128], P(('col', 'row')), may hold values from -0.0625 to 0.0625
- factor_c: float32 [12, 128], replicated, may hold values from -1.75 to 1.75
Outputs:
- a_update: float32 [8192, 128], P(('row', 'col'))
- b_update: float32 [8192, 128], P(('col', 'row'))
All inputs are finite; a program needn't handle non-finite values.
Results may differ from a plain program's by a relative error of at most 0.00012.
Values sent between devices are 32-bit elements; how exact they have to be, the bound alone decides.
No kernel may reach another device: no remote copies, remote signals or barrier semaphores. Data moves between devices by JAX's collectives and lax.ppermute only.
A program may use at most 64 MiB of HBM per device.

v0:
```python
import jax
import jax.numpy as jnp
from jax import lax
from jax.sharding import PartitionSpec as P

EPSILON = 1e-06


def solve_system(rhs, system):
    highest = lax.Precision.HIGHEST
    lower = jnp.linalg.cholesky(system)
    inverse = jax.scipy.linalg.cho_solve(
        (lower, True), jnp.eye(system.shape[0], dtype=system.dtype)
    )
    return jnp.dot(rhs, inverse, precision=highest)


def gram_of(matrix):
    return jnp.dot(matrix.T, matrix, precision=lax.Precision.HIGHEST)


def per_device(tensor, factor_b, factor_c):
    highest = lax.Precision.HIGHEST
    rows_block = tensor.shape[1]
    cols_block = tensor.shape[2]
    rank_width = factor_c.shape[1]
    owned_a = rows_block // lax.axis_size("col")
    owned_b = cols_block // lax.axis_size("row")
    c_gram = gram_of(factor_c)
    empty_b = jnp.zeros((cols_block, rank_width), jnp.float32)
    gram_b = lax.psum(gram_of(factor_b), ("row", "col"))
    block = tensor
    khatri = factor_c[:, None, :] * lax.all_gather(factor_b, "row", axis=0, tiled=True)[None, :, :]
    partial_a = jnp.einsum("kij,kjr->ir", block, khatri, precision=highest)
    whole_a = lax.psum(partial_a, "col")
    summed_a = lax.dynamic_slice_in_dim(whole_a, lax.axis_index("col") * owned_a, owned_a, 0)
    a_update = solve_system(summed_a, c_gram * gram_b)
    squares = lax.psum(jnp.sum(a_update * a_update, axis=0), ("row", "col"))
    factor_a = a_update / jnp.sqrt(squares + EPSILON)
    gram_a = lax.psum(gram_of(factor_a), ("row", "col"))
    block = tensor
    khatri = factor_c[:, None, :] * lax.all_gather(factor_a, "col", axis=0, tiled=True)[None, :, :]
    partial_b = empty_b + jnp.einsum("kij,kir->jr", block, khatri, precision=highest)
    whole_b = lax.psum(partial_b, "row")
    summed_b = lax.dynamic_slice_in_dim(whole_b, lax.axis_index("row") * owned_b, owned_b, 0)
    b_update = solve_system(summed_b, c_gram * gram_a)
    return (a_update, b_update)


def solution(mesh):
    placed = (P(None, "row", "col"), P(("col", "row"), None), P())
    return jax.shard_map(
        per_device,
        mesh=mesh,
        in_specs=placed,
        out_specs=(P(("row", "col"), None), P(("col", "row"), None)),
        check_vma=False,
    )
```

profile of v0, /device:TPU:1, one launch (start us, length us, event | category | flops | bytes accessed | tf_op | source)
XLA Modules:
  0.0 809.7 jit_solution(5450451104905007428)
XLA Ops:
  7.2 1.7 fusion.35
  9.0 22.3 %all_gather.6 = f32[512,128]{1,0:T(8,128)S(1)} all-gather(f32[32,128]{1,0:T(8,128)} %param.7), channel_id=1, replica_groups=mesh['row'=16,'col'=16] {'row'}, dimensions={0}, use_global_device_ids=true | all-gather | bytes 278528 | tf_op jit(solution)/shard_map/all_gather | solution.py:33
  31.2 18.3 %fusion.8 = f32[512,128]{0,1:T(8,128)} fusion(f32[12,512,512]{2,1,0:T(8,128)} %param.6, f32[512,128]{1,0:T(8,128)S(1)} %all_gather.6, f32[12,128]{1,0:T(8,128)} %param.8), kind=kOutput, calls=%fused_computation.8 | convolution fusion | flops 4832624640 | bytes 13113344 | tf_op jit(solution)/shard_map/kij,kjr->ir/dot_general | solution.py:34
  49.8 209.2 %all-reduce.7.cloned.1.call-done = f32[128,128]{0,1:T(8,128)} async-done(((f32[128,128]{0,1:T(8,128)}), f32[128,128]{0,1:T(8,128)}) %all-reduce.7.cloned.1.call-update) | async-done | bytes 65552 | tf_op jit(solution)/shard_map/psum | solution.py:31
  259.1 1.1 fusion.34
  260.3 11.7 %cholesky.44 = f32[128,128]{1,0:T(8,128)S(1)} custom-call(f32[128,128]{1,0:T(8,128)S(1)} %fusion.27), custom_call_target="Cholesky" | custom-call | tf_op jit(solution)/shard_map/jit(cholesky)/cholesky | solution.py:11
  272.1 0.6 compare_reduce_fusion.1
  272.7 0.7 fusion.18
  273.4 9.8 %custom-call.8 = f32[1,128,128]{1,2,0:T(8,128)S(1)} custom-call(f32[1,128,128]{2,1,0:T(8,128)S(1)} %fusion.18), custom_call_target="InvertDiagBlocksLowerTriangular" | custom-call | tf_op jit(solution)/shard_map/jit(_cho_solve)/triangular_solve | solution.py:12
  283.2 0.3 fusion.16
  283.7 68.0 %all-reduce.5.cloned.1.call-done = f32[512,128]{0,1:T(8,128)} async-done(((f32[512,128]{0,1:T(8,128)}), f32[512,128]{0,1:T(8,128)}) %all-reduce.5.cloned.1.call-update) | async-done | bytes 262160 | tf_op jit(solution)/shard_map/psum | solution.py:35
  351.7 1.2 multiply_reduce_fusion
  352.8 77.5 %psum.37 = f32[128]{0:T(128)S(1)} all-reduce(f32[128]{0:T(128)S(1)} %get-tuple-element.6), channel_id=1, replica_groups=mesh['row'=16,'col'=16] {'row','col'}, use_global_device_ids=true, to_apply=%region_5.0 | all-reduce | flops 128 | bytes 1024 | tf_op jit(solution)/shard_map/psum | solution.py:38
  430.3 0.9 fusion.36
  431.3 15.8 %all_gather.7 = f32[512,128]{1,0:T(8,128)S(1)} all-gather(f32[32,128]{1,0:T(8,128)S(1)} %broadcast_divide_fusion), channel_id=1, replica_groups=mesh['row'=16,'col'=16] {'col'}, dimensions={0}, use_global_device_ids=true | all-gather | bytes 278528 | tf_op jit(solution)/shard_map/all_gather | solution.py:42
  447.3 11.4 %fusion.11 = f32[512,128]{0,1:T(8,128)} fusion(f32[12,512,512]{2,1,0:T(8,128)} %param.6, f32[512,128]{1,0:T(8,128)S(1)} %all_gather.7, f32[12,128]{1,0:T(8,128)S(1)} %copy-done), kind=kOutput, calls=%fused_computation.9 | convolution fusion | flops 4832624640 | bytes 13113344 | tf_op jit(solution)/shard_map/kij,kir->jr/dot_general | solution.py:43
  458.8 234.0 %all-reduce.11.cloned.1.call-done = f32[128,128]{0,1:T(8,128)} async-done(((f32[128,128]{0,1:T(8,128)}), f32[128,128]{0,1:T(8,128)}) %all-reduce.11.cloned.1.call-update) | async-done | bytes 65552 | tf_op jit(solution)/shard_map/psum | solution.py:40
  692.8 0.9 mul.48
  693.8 11.7 %cholesky.55 = f32[128,128]{1,0:T(8,128)S(1)} custom-call(f32[128,128]{1,0:T(8,128)S(1)} %fusion.23), custom_call_target="Cholesky" | custom-call | tf_op jit(solution)/shard_map/jit(cholesky)/cholesky | solution.py:11
  705.5 0.6 compare_reduce_fusion
  706.2 0.7 fusion.19
  706.8 9.8 %custom-call.9 = f32[1,128,128]{1,2,0:T(8,128)S(1)} custom-call(f32[1,128,128]{2,1,0:T(8,128)S(1)} %fusion.19), custom_call_target="InvertDiagBlocksLowerTriangular" | custom-call | tf_op jit(solution)/shard_map/jit(_cho_solve)/triangular_solve | solution.py:12
  717.2 84.3 %all-reduce.9.cloned.1.call-done = f32[512,128]{0,1:T(8,128)} async-done(((f32[512,128]{0,1:T(8,128)}), f32[512,128]{0,1:T(8,128)}) %all-reduce.9.cloned.1.call-update) | async-done | bytes 262160 | tf_op jit(solution)/shard_map/psum | solution.py:44
  801.4 1.8 fusion.28
  (23 shorter events, 1.6 us)
Async XLA Ops:
  7.2 251.9 %all-reduce.7.cloned.1.call-start = ((), (), s32[]{:S(2)}) async-start(), calls=%async_computation.1 | async-start | bytes 131072 | tf_op jit(solution)/shard_map/psum | solution.py:31
  8.9 342.7 %all-reduce.5.cloned.1.call-start = ((), (), s32[]{:S(2)}) async-start(), calls=%async_computation | async-start | bytes 524288 | tf_op jit(solution)/shard_map/psum | solution.py:35
  31.2 227.8 %copy-start = (f32[12,128]{1,0:T(8,128)S(1)}, f32[12,128]{1,0:T(8,128)}, u32[]{:S(2)}) copy-start(f32[12,128]{1,0:T(8,128)} %param.8) | copy-start | bytes 18436
  49.6 643.2 %all-reduce.11.cloned.1.call-start = ((), (), s32[]{:S(2)}) async-start(), calls=%async_computation.3 | async-start | bytes 131072 | tf_op jit(solution)/shard_map/psum | solution.py:40
  352.8 105.9 %copy-start.1 = (f32[32,128]{1,0:T(8,128)}, f32[32,128]{1,0:T(8,128)S(1)}, u32[]{:S(2)}) copy-start(f32[32,128]{1,0:T(8,128)S(1)} %get-tuple-element.7) | copy-start | bytes 49156
  447.1 354.4 %all-reduce.9.cloned.1.call-start = ((), (), s32[]{:S(2)}) async-start(), calls=%async_computation.2 | async-start | bytes 524288 | tf_op jit(solution)/shard_map/psum | solution.py:44
Sparse Core Ops, SparseCore 0:
  13.5 245.5 all-reduce.6
  262.2 89.3 all-reduce.4
  447.2 245.5 all-reduce.10
  695.0 106.4 all-reduce.8
where the time goes:
time: 810 us
  waiting for transfers between devices  596 us (74%)
  blocking collectives  116 us (14%)
  other arithmetic  46.6 us (6%)
  matrix products  37.4 us (5%)
  between operations  13.9 us (2%)
    psum x1, waiting for transfers between devices, per_device(): gram_a = lax.psum(gram_of(factor_a), ('row', 'col'))  234 us
    psum x1, waiting for transfers between devices, per_device(): gram_b = lax.psum(gram_of(factor_b), ('row', 'col'))  209 us
    psum x1, waiting for transfers between devices, per_device(): whole_b = lax.psum(partial_b, 'row')  84.3 us
    psum x1, blocking collectives, per_device(): squares = lax.psum(jnp.sum(a_update * a_update, axis=0), ('row', 'col'))  77.5 us
    psum x1, waiting for transfers between devices, per_device(): whole_a = lax.psum(partial_a, 'col')  68 us
    another operation x6, other arithmetic, solve_system(): lower = jnp.linalg.cholesky(system)  24.8 us
    all_gather x1, blocking collectives, per_device(): lax.all_gather(factor_b, 'row', axis=0, tiled=True)[None, :, :]  22.3 us
    another operation x4, other arithmetic, solve_system(): jax.scipy.linalg.cho_solve((lower, True), jnp.eye(system.shape[0], dtype=...  20.9 us
  transfers between devices with their start and end apart: 4, of which 4 were waited for; matrix products, arithmetic and copies ran while one was open for 10% of the time, Pallas kernels for 0%

commit v1 on v0

v1 whole, which is shorter than its diff:
```python
import functools

import jax
import jax.numpy as jnp
from jax import lax
from jax.experimental import pallas as pl
from jax.experimental.pallas import tpu as pltpu
from jax.sharding import Mesh
from jax.sharding import PartitionSpec as P

EPSILON = 1e-06
HIGHEST = lax.Precision.HIGHEST
VMEM = pl.BlockSpec(memory_space=pltpu.VMEM)
ANY = pl.BlockSpec(memory_space=pl.ANY)
SMEM = pl.BlockSpec(memory_space=pltpu.SMEM)
ROW = ("z", "core")
COL = ("x", "y")


def split(value):
    high = value.astype(jnp.bfloat16)
    low = (value - high.astype(jnp.float32)).astype(jnp.bfloat16)
    return high, low


def contract_rows(left, right):
    return lax.dot_general(
        left, right, (((0,), (0,)), ((), ())), precision=HIGHEST,
        preferred_element_type=jnp.float32,
    )


def dot32(left, right):
    return lax.dot_general(
        left, right, (((1,), (0,)), ((), ())), precision=HIGHEST,
        preferred_element_type=jnp.float32,
    )


def inverse(system):
    size = system.shape[0]
    lanes = lax.broadcasted_iota(jnp.int32, (1, size), 1)
    rows = lax.broadcasted_iota(jnp.int32, (size, 1), 0)
    matrix = system
    for k in range(size):
        pivot = 1.0 / matrix[k : k + 1, k : k + 1]
        row = jnp.where(lanes == k, pivot, matrix[k : k + 1, :] * pivot)
        column = jnp.where(rows == k, 0.0, matrix[:, k : k + 1])
        kept = jnp.where(lanes == k, 0.0, matrix)
        matrix = jnp.where(rows == k, row, kept - column * row)
    return matrix


def first_kernel(t_hbm, b_ref, c_ref, out_ref, t_buf, b_both, total, sems):
    slices = t_hbm.shape[0]
    for k in range(slices):
        pltpu.make_async_copy(t_hbm.at[k], t_buf.at[k], sems.at[k]).start()
    factor = b_ref[...]
    width = factor.shape[1]
    b_high, b_low = split(factor)
    b_both[:, :width] = b_high
    b_both[:, width:] = b_low
    gram = contract_rows(factor, factor)
    parts, rows, _ = out_ref.shape
    share = width // parts
    out_ref[:, rows - share :, :] = gram.reshape(parts, share, width)
    for k in range(slices):
        pltpu.make_async_copy(t_hbm.at[k], t_buf.at[k], sems.at[k]).wait()
        t_high, t_low = split(t_buf[k])
        main = jnp.dot(t_high, b_both[...], preferred_element_type=jnp.float32)
        rest = jnp.dot(t_low, b_both[:, :width], preferred_element_type=jnp.float32)
        term = (main[:, :width] + (main[:, width:] + rest)) * c_ref[k : k + 1, :]
        if k == 0:
            total[...] = term
        else:
            total[...] += term
    out_ref[:, : rows - share, :] = total[...].reshape(parts, rows - share, width)


def middle_kernel(where_ref, g_ref, c_ref, a_ref, scaled_ref, message_ref, block):
    parts, rows, width = g_ref.shape
    share = width // parts
    owned = rows - share
    factor_c = c_ref[...]
    system = contract_rows(factor_c, factor_c) * g_ref[:, owned:, :].reshape(width, width)
    solved = inverse(system)
    update = dot32(g_ref[:, :owned, :].reshape(parts * owned, width), solved)
    block[...] = update
    start = pl.multiple_of(where_ref[0] * owned, owned)
    a_ref[...] = block[pl.ds(start, owned), :]
    most = jnp.max(jnp.abs(update), axis=0, keepdims=True)
    most = jnp.where(most > 0.0, most, 1.0)
    scaled = update / most
    scaled_ref[...] = scaled
    gram = contract_rows(update, scaled)
    targets, height, _ = message_ref.shape
    piece = width // targets
    message_ref[:, :piece, :] = gram.reshape(targets, piece, width)
    message_ref[:, piece:, :] = jnp.broadcast_to(
        most.reshape(1, 1, width), (targets, height - piece, width)
    )


def second_kernel(t_hbm, scaled_ref, c_ref, out_ref, t_buf, total, sems):
    slices = t_hbm.shape[0]
    for k in range(slices):
        pltpu.make_async_copy(t_hbm.at[k], t_buf.at[k], sems.at[k]).start()
    turned = scaled_ref[...].T
    width = turned.shape[0]
    c_turned = c_ref[...].T
    for k in range(slices):
        w_high, w_low = split(turned * c_turned[:, k : k + 1])
        w_both = jnp.concatenate([w_high, w_low], axis=0)
        pltpu.make_async_copy(t_hbm.at[k], t_buf.at[k], sems.at[k]).wait()
        t_high, t_low = split(t_buf[k])
        main = jnp.dot(w_both, t_high, preferred_element_type=jnp.float32)
        rest = jnp.dot(w_high, t_low, preferred_element_type=jnp.float32)
        term = main[:width] + (main[width:] + rest)
        if k == 0:
            total[...] = term
        else:
            total[...] += term
    out_ref[...] = total[...].T.reshape(out_ref.shape)


def combine_kernel(message_ref, chunk_ref, scale_ref):
    senders, height, width = message_ref.shape
    piece = chunk_ref.shape[0]
    all_most = message_ref[:, piece, :]
    most = jnp.max(all_most, axis=0, keepdims=True)
    scales = all_most / most
    chunk = jnp.zeros(chunk_ref.shape, jnp.float32)
    for d in range(senders):
        chunk += message_ref[d, :piece, :] * scales[d : d + 1, :]
    chunk_ref[...] = chunk
    scale_ref[:senders, :] = scales
    scale_ref[senders:, :] = jnp.broadcast_to(most, (scale_ref.shape[0] - senders, width))


def last_kernel(parts_ref, h_ref, scale_ref, c_ref, out_ref):
    senders, owned, width = parts_ref.shape
    scales = scale_ref[:senders, :]
    most = scale_ref[senders : senders + 1, :]
    total = jnp.zeros((owned, width), jnp.float32)
    for d in range(senders):
        total += parts_ref[d] * scales[d : d + 1, :]
    gram = h_ref[...].reshape(width, width)
    same = lax.broadcasted_iota(jnp.int32, (width, width), 0) == lax.broadcasted_iota(
        jnp.int32, (width, width), 1
    )
    norms = jnp.sqrt(jnp.sum(jnp.where(same, gram, 0.0), axis=0, keepdims=True) * most + EPSILON)
    ratio = most / norms
    flipped = jnp.sum(jnp.where(same, jnp.broadcast_to(norms, (width, width)), 0.0), axis=1, keepdims=True)
    factor_c = c_ref[...]
    system = contract_rows(factor_c, factor_c) * ((gram * ratio) / flipped)
    out_ref[...] = dot32(total * ratio, inverse(system))


def per_device(tensor, factor_b, factor_c):
    slices, rows_block, cols_block = tensor.shape
    width = factor_c.shape[1]
    row_size = lax.axis_size(ROW)
    col_size = lax.axis_size(COL)
    owned_a = rows_block // col_size
    owned_b = cols_block // row_size
    share_a = width // col_size
    share_b = width // row_size
    f32 = jnp.float32
    params = pltpu.CompilerParams(vmem_limit_bytes=48 * 1024 * 1024)

    b_block = lax.all_gather(factor_b, ROW, axis=0, tiled=True)
    packed = pl.pallas_call(
        first_kernel,
        out_shape=jax.ShapeDtypeStruct((col_size, owned_a + share_a, width), f32),
        in_specs=[ANY, VMEM, VMEM],
        out_specs=VMEM,
        scratch_shapes=[
            pltpu.VMEM((slices, rows_block, cols_block), f32),
            pltpu.VMEM((cols_block, 2 * width), jnp.bfloat16),
            pltpu.VMEM((rows_block, width), f32),
            pltpu.SemaphoreType.DMA((slices,)),
        ],
        compiler_params=params,
        name="first",
    )(tensor, b_block, factor_c)
    received = lax.all_to_all(packed, COL, 0, 0, tiled=True)
    summed = jnp.sum(received, axis=0)
    gathered = lax.all_to_all(
        jnp.broadcast_to(summed[None], received.shape), COL, 0, 0, tiled=True
    )
    where = lax.axis_index(COL).astype(jnp.int32).reshape(1)
    a_update, scaled, message = pl.pallas_call(
        middle_kernel,
        out_shape=(
            jax.ShapeDtypeStruct((owned_a, width), f32),
            jax.ShapeDtypeStruct((rows_block, width), f32),
            jax.ShapeDtypeStruct((row_size, share_b + 8, width), f32),
        ),
        in_specs=[SMEM, VMEM, VMEM],
        out_specs=(VMEM, VMEM, VMEM),
        scratch_shapes=[pltpu.VMEM((rows_block, width), f32)],
        name="middle",
    )(where, gathered, factor_c)
    grams = lax.all_to_all(message, ROW, 0, 0, tiled=True)
    partial_b = pl.pallas_call(
        second_kernel,
        out_shape=jax.ShapeDtypeStruct((row_size, owned_b, width), f32),
        in_specs=[ANY, VMEM, VMEM],
        out_specs=VMEM,
        scratch_shapes=[
            pltpu.VMEM((slices, rows_block, cols_block), f32),
            pltpu.VMEM((width, cols_block), f32),
            pltpu.SemaphoreType.DMA((slices,)),
        ],
        compiler_params=params,
        cost_estimate=pl.CostEstimate(
            flops=6 * slices * rows_block * cols_block * width,
            bytes_accessed=4 * slices * rows_block * cols_block,
            transcendentals=0,
        ),
        name="second",
    )(tensor, scaled, factor_c)
    chunk, scales = pl.pallas_call(
        combine_kernel,
        out_shape=(
            jax.ShapeDtypeStruct((share_b, width), f32),
            jax.ShapeDtypeStruct((row_size + 8, width), f32),
        ),
        in_specs=[VMEM],
        out_specs=(VMEM, VMEM),
        name="combine",
    )(grams)
    outgoing = jnp.concatenate(
        [partial_b, jnp.broadcast_to(chunk[None], (row_size,) + chunk.shape)], axis=1
    )
    final = lax.all_to_all(outgoing, ROW, 0, 0, tiled=True)
    b_update = pl.pallas_call(
        last_kernel,
        out_shape=jax.ShapeDtypeStruct((owned_b, width), f32),
        in_specs=[VMEM] * 4,
        out_specs=VMEM,
        name="last",
    )(final[:, :owned_b, :], final[:, owned_b:, :], scales, factor_c)
    return (a_update, b_update)


def solution(mesh):
    finer = Mesh(mesh.devices.reshape(8, 2, 4, 4), ("z", "core", "x", "y"))
    placed = (P(None, ROW, COL), P(COL + ROW, None), P())
    return jax.shard_map(
        per_device,
        mesh=finer,
        in_specs=placed,
        out_specs=(P(ROW + COL, None), P(COL + ROW, None)),
        check_vma=False,
    )
```

time: 810 us -> 123 us (0.15)
  waiting for transfers between devices: 596 us -> 10.4 us
  blocking collectives: 116 us -> 54.2 us
  other arithmetic: 46.6 us -> 0.05 us
  Pallas kernels: 0 us -> 40.8 us
  matrix products: 37.4 us -> 0 us
  between operations: 13.9 us -> 0.69 us
  starting transfers between devices: 0.57 us -> 10.4 us
    psum x4 -> x0, waiting for transfers between devices: 595 us -> none  [the longest x1 234 us: per_device(): gram_a = lax.psum(gram_of(factor_a), ('row', 'col'))]
    psum x1 -> x0, blocking collectives: 77.5 us -> none  [per_device(): squares = lax.psum(jnp.sum(a_update * a_update, axis=0), ('row', 'col'))]
    another operation x10 -> x0, other arithmetic: 45.7 us -> none  [the longest x6 24.8 us: solve_system(): lower = jnp.linalg.cholesky(system)]
    pallas_call x0 -> x5, Pallas kernels: none -> 40.8 us  [the longest x1 14 us: per_device(): pl.pallas_call(middle_kernel, out_shape=(jax.ShapeDtypeStruct((owned_a, w...]
    dot_general x7 -> x0, matrix products: 36.4 us -> none  [the longest x1 18.3 us: per_device(): partial_a = jnp.einsum('kij,kjr->ir', block, khatri, precision=highest)]
    all_to_all x0 -> x2, blocking collectives: none -> 32 us  [the longest x1 17.3 us: per_device(): final = lax.all_to_all(outgoing, ROW, 0, 0, tiled=True)]
    all_gather x2 -> x1, blocking collectives: 38 us -> 22.3 us  [per_device(): b_block = lax.all_gather(factor_b, ROW, axis=0, tiled=True)]
    all_to_all x0 -> x2, waiting for transfers between devices: none -> 10.4 us  [the longest x1 7.71 us: per_device(): lax.all_to_all(jnp.broadcast_to(summed[None], received.shape), COL, 0, 0,...]
  transfers between devices with their start and end apart: 4 -> 2, of which waited for: 4 -> 2; matrix products, arithmetic and copies ran while one was open for 10% -> 0% of each run, Pallas kernels for 0% -> 4%
where the time goes in v1:
time: 123 us; the launch traced here: 122 us
  blocking collectives  54.2 us (44%)
  Pallas kernels  40.8 us (33%)
  starting transfers between devices  10.4 us (8%)
  waiting for transfers between devices  10.4 us (8%)
  local copies, waits for them, and re-layouts  5.8 us (5%)
    all_gather x1, blocking collectives, per_device(): b_block = lax.all_gather(factor_b, ROW, axis=0, tiled=True)  22.3 us
    all_to_all x1, blocking collectives, per_device(): final = lax.all_to_all(outgoing, ROW, 0, 0, tiled=True)  17.3 us
    all_to_all x1, blocking collectives, per_device(): received = lax.all_to_all(packed, COL, 0, 0, tiled=True)  14.7 us
    pallas_call x1, Pallas kernels, per_device(): pl.pallas_call(middle_kernel, out_shape=(jax.ShapeDtypeStruct((owned_a, w...  14 us
    pallas_call x1, Pallas kernels, per_device(): pl.pallas_call(last_kernel, out_shape=jax.ShapeDtypeStruct((owned_b, widt...  13.2 us
    all_to_all x1, waiting for transfers between devices, per_device(): lax.all_to_all(jnp.broadcast_to(summed[None], received.shape), COL, 0, 0,...  7.71 us
    pallas_call x1, Pallas kernels, per_device(): pl.pallas_call(first_kernel, out_shape=jax.ShapeDtypeStruct((col_size, ow...  6.86 us
    all_to_all x1, starting transfers between devices, per_device(): grams = lax.all_to_all(message, ROW, 0, 0, tiled=True)  6.33 us
  transfers between devices with their start and end apart: 2, of which 2 were waited for; matrix products, arithmetic and copies ran while one was open for 0% of the time, Pallas kernels for 4%

profile of v1, /device:TPU:1, one launch (start us, length us, event | category | flops | bytes accessed | tf_op | source)
XLA Modules:
  0.0 122.4 jit_solution(14488411407748231484)
XLA Ops:
  0.6 0.0 copy-start.2
  0.6 22.3 %all_gather.3.b_ref = f32[512,128]{1,0:T(8,128)S(1)} all-gather(f32[32,128]{1,0:T(8,128)} %param.4), channel_id=1, replica_groups=mesh['z'=8,'core'=2,'x'=4,'y'=4] {'z','core'}, dimensions={0}, use_global_device_ids=true | all-gather | bytes 278528 | tf_op jit(solution)/shard_map/all_gather | solution.py:171
  22.9 0.0 copy-start.1
  22.9 0.7 copy-done.1
  23.6 6.9 %first.1 = f32[16,40,128]{2,1,0:T(8,128)S(1)} custom-call(f32[12,512,512]{2,1,0:T(8,128)} %t_hbm.3, f32[512,128]{1,0:T(8,128)S(1)} %all_gather.3.b_ref, f32[12,128]{1,0:T(8,128)S(1)} %copy-done.1), custom_call_target="tpu_custom_call" | custom-call | tf_op jit(solution)/shard_map/first/pallas_call | solution.py:172
  30.5 14.7 %all_to_all.20 = f32[16,40,128]{2,1,0:T(8,128)S(1)} all-to-all(f32[16,40,128]{2,1,0:T(8,128)S(1)} %first.1), channel_id=1, replica_groups=mesh['z'=8,'core'=2,'x'=4,'y'=4] {'x','y'}, dimensions={0} | all-to-all | bytes 655360 | tf_op jit(solution)/shard_map/all_to_all | solution.py:186
  45.2 0.7 broadcast_in_dim.4
  46.0 4.0 %all-to-all-start.1 = ((f32[16,40,128]{2,1,0:T(8,128)}), f32[16,40,128]{2,1,0:T(8,128)S(1)}, u32[]{:S(2)}, u32[]{:S(2)}) async-start(f32[16,40,128]{2,1,0:T(8,128)} %broadcast_in_dim.4), calls=%async_computation.1 | async-start | bytes 655360 | tf_op jit(solution)/shard_map/all_to_all | solution.py:188
  50.0 7.7 %all-to-all-done.1.g_ref = f32[16,40,128]{2,1,0:T(8,128)S(1)} async-done(((f32[16,40,128]{2,1,0:T(8,128)}), f32[16,40,128]{2,1,0:T(8,128)S(1)}, u32[]{:S(2)}, u32[]{:S(2)}) %all-to-all-start.1) | async-done | bytes 327712 | tf_op jit(solution)/shard_map/all_to_all | solution.py:188
  57.7 0.7 copy-done.3
  58.4 14.0 %middle.1 = (f32[32,128]{1,0:T(8,128)}, f32[512,128]{1,0:T(8,128)}, f32[16,16,128]{2,1,0:T(8,128)}) custom-call(s32[1]{0:T(128)} %bitcast.where_ref, f32[16,40,128]{2,1,0:T(8,128)} %copy-done.3, f32[12,128]{1,0:T(8,128)} %c_ref.7), custom_call_target="tpu_custom_call" | custom-call | tf_op jit(solution)/shard_map/middle/pallas_call | solution.py:192
  72.5 6.3 %all-to-all-start.2 = ((f32[16,16,128]{2,1,0:T(8,128)}), f32[16,16,128]{2,1,0:T(8,128)S(1)}, u32[]{:S(2)}, u32[]{:S(2)}) async-start(f32[16,16,128]{2,1,0:T(8,128)} %get-tuple-element.9), calls=%async_computation.2 | async-start | bytes 262144 | tf_op jit(solution)/shard_map/all_to_all | solution.py:204
  78.8 0.0 copy-done.2
  78.8 0.0 copy-start
  78.8 0.9 copy-done
  79.8 5.2 %second.1 = f32[16,32,128]{2,1,0:T(8,128)S(1)} custom-call(f32[12,512,512]{2,1,0:T(8,128)} %t_hbm.3, f32[512,128]{1,0:T(8,128)S(1)} %copy-done, f32[12,128]{1,0:T(8,128)S(1)} %copy-done.2), custom_call_target="tpu_custom_call" | custom-call | flops 2415919104 | bytes 12582912 | tf_op jit(solution)/shard_map/second/pallas_call | solution.py:205
  85.0 2.7 %all-to-all-done.2.message_ref = f32[16,16,128]{2,1,0:T(8,128)S(1)} async-done(((f32[16,16,128]{2,1,0:T(8,128)}), f32[16,16,128]{2,1,0:T(8,128)S(1)}, u32[]{:S(2)}, u32[]{:S(2)}) %all-to-all-start.2) | async-done | bytes 131104 | tf_op jit(solution)/shard_map/all_to_all | solution.py:204
  87.7 0.6 copy-done.4
  88.4 1.5 %combine.1 = (f32[8,128]{1,0:T(8,128)}, f32[24,128]{1,0:T(8,128)}) custom-call(f32[16,16,128]{2,1,0:T(8,128)} %copy-done.4), custom_call_target="tpu_custom_call" | custom-call | tf_op jit(solution)/shard_map/combine/pallas_call | solution.py:223
  89.9 0.7 broadcast_in_dim.5
  90.6 17.3 %all_to_all.21 = f32[16,40,128]{2,1,0:T(8,128)S(1)} all-to-all(f32[16,40,128]{2,1,0:T(8,128)S(1)} %pad_maximum_fusion), channel_id=1, replica_groups=mesh['z'=8,'core'=2,'x'=4,'y'=4] {'z','core'}, dimensions={0} | all-to-all | bytes 655360 | tf_op jit(solution)/shard_map/all_to_all | solution.py:236
  107.9 0.6 slice.9.h_ref
  108.5 0.7 slice.8.parts_ref
  109.2 13.2 %last.1 = f32[32,128]{1,0:T(8,128)} custom-call(f32[16,32,128]{2,1,0:T(8,128)} %slice.8.parts_ref, f32[16,8,128]{2,1,0:T(8,128)} %slice.9.h_ref, f32[24,128]{1,0:T(8,128)} %get-tuple-element.11.scale_ref, f32[12,128]{1,0:T(8,128)} %c_ref.7), custom_call_target="tpu_custom_call" | custom-call | tf_op jit(solution)/shard_map/last/pallas_call | solution.py:237
  (4 shorter events, 0.1 us)
Async XLA Ops:
  0.6 78.2 %copy-start.2 = (f32[12,128]{1,0:T(8,128)S(1)}, f32[12,128]{1,0:T(8,128)}, u32[]{:S(2)}) copy-start(f32[12,128]{1,0:T(8,128)} %c_ref.7) | copy-start | bytes 18436
  22.9 0.7 copy-start.1
  46.0 11.8 %all-to-all-start.1 = ((f32[16,40,128]{2,1,0:T(8,128)}), f32[16,40,128]{2,1,0:T(8,128)S(1)}, u32[]{:S(2)}, u32[]{:S(2)}) async-start(f32[16,40,128]{2,1,0:T(8,128)} %broadcast_in_dim.4), calls=%async_computation.1 | async-start | bytes 655360 | tf_op jit(solution)/shard_map/all_to_all | solution.py:188
  57.7 0.7 copy-start.3
  72.5 15.2 %all-to-all-start.2 = ((f32[16,16,128]{2,1,0:T(8,128)}), f32[16,16,128]{2,1,0:T(8,128)S(1)}, u32[]{:S(2)}, u32[]{:S(2)}) async-start(f32[16,16,128]{2,1,0:T(8,128)} %get-tuple-element.9), calls=%async_computation.2 | async-start | bytes 262144 | tf_op jit(solution)/shard_map/all_to_all | solution.py:204
  78.8 1.0 copy-start
  87.7 0.7 copy-start.4

commit v2 on v1

--- a/solution.py
+++ b/solution.py
@@ -1,5 +1,3 @@
-import functools
-
 import jax
 import jax.numpy as jnp
 from jax import lax
@@ -11,10 +9,12 @@
 EPSILON = 1e-06
 HIGHEST = lax.Precision.HIGHEST
 VMEM = pl.BlockSpec(memory_space=pltpu.VMEM)
-ANY = pl.BlockSpec(memory_space=pl.ANY)
+HBM = pl.BlockSpec(memory_space=pltpu.HBM)
 SMEM = pl.BlockSpec(memory_space=pltpu.SMEM)
 ROW = ("z", "core")
 COL = ("x", "y")
+LARGE_MIB = 52
+WORK_MIB = 12
 
 
 def split(value):
@@ -39,24 +39,73 @@
 
 def inverse(system):
     size = system.shape[0]
-    lanes = lax.broadcasted_iota(jnp.int32, (1, size), 1)
-    rows = lax.broadcasted_iota(jnp.int32, (size, 1), 0)
-    matrix = system
-    for k in range(size):
-        pivot = 1.0 / matrix[k : k + 1, k : k + 1]
-        row = jnp.where(lanes == k, pivot, matrix[k : k + 1, :] * pivot)
-        column = jnp.where(rows == k, 0.0, matrix[:, k : k + 1])
-        kept = jnp.where(lanes == k, 0.0, matrix)
-        matrix = jnp.where(rows == k, row, kept - column * row)
-    return matrix
-
-
-def first_kernel(t_hbm, b_ref, c_ref, out_ref, t_buf, b_both, total, sems):
+    lane = lax.broadcasted_iota(jnp.int32, (8, size), 1)
+    sublane = lax.broadcasted_iota(jnp.int32, (8, size), 0)
+
+    def spread(value):
+        return jnp.broadcast_to(value, (8, size))
+
+    strips = [system[8 * i : 8 * i + 8, :] for i in range(size // 8)]
+    for c in range(size // 8):
+        first = 8 * c
+        columns = [spread(strips[c][:, first + j : first + j + 1]) for j in range(8)]
+        entry = {(i, j): spread(columns[j][i : i + 1, :]) for j in range(8) for i in range(j + 1)}
+
+        def key(i, j):
+            return (i, j) if i <= j else (j, i)
+
+        for k in range(8):
+            pivot = 1.0 / entry[k, k]
+            old = [entry[key(i, k)] for i in range(8)]
+            part = [value * pivot for value in old]
+            for i in range(8):
+                for j in range(i, 8):
+                    if i != k and j != k:
+                        entry[i, j] = entry[i, j] - part[i] * old[j]
+            for i in range(8):
+                entry[key(i, k)] = -pivot if i == k else part[i]
+        inside = (lane >= first) & (lane < first + 8)
+        rows = [
+            jnp.where(
+                inside,
+                jnp.where(lane == first + j, 1.0, 0.0),
+                spread(strips[c][j : j + 1, :]),
+            )
+            for j in range(8)
+        ]
+        minus = []
+        for i in range(8):
+            terms = [entry[key(i, j)] * rows[j] for j in range(8)]
+            minus.append(
+                ((terms[0] + terms[1]) + (terms[2] + terms[3]))
+                + ((terms[4] + terms[5]) + (terms[6] + terms[7]))
+            )
+        for m in range(size // 8):
+            if m == c:
+                continue
+            terms = [
+                spread(strips[m][:, first + j : first + j + 1]) * minus[j] for j in range(8)
+            ]
+            strips[m] = jnp.where(inside, 0.0, strips[m]) + (
+                ((terms[0] + terms[1]) + (terms[2] + terms[3]))
+                + ((terms[4] + terms[5]) + (terms[6] + terms[7]))
+            )
+        solved = minus[0]
+        for i in range(1, 8):
+            solved = jnp.where(sublane == i, minus[i], solved)
+        strips[c] = -solved
+    return jnp.concatenate(strips, axis=0)
+
+
+def first_kernel(core_ref, t_hbm, mine_ref, other_ref, c_ref, out_ref, t_buf, b_block, b_both, total, sems):
     slices = t_hbm.shape[0]
     for k in range(slices):
         pltpu.make_async_copy(t_hbm.at[k], t_buf.at[k], sems.at[k]).start()
-    factor = b_ref[...]
-    width = factor.shape[1]
+    core = core_ref[0]
+    b_block[:, core] = mine_ref[...]
+    b_block[:, 1 - core] = other_ref[...]
+    width = c_ref.shape[1]
+    factor = b_block[...].reshape(b_both.shape[0], width)
     b_high, b_low = split(factor)
     b_both[:, :width] = b_high
     b_both[:, width:] = b_low
@@ -75,6 +124,14 @@
         else:
             total[...] += term
     out_ref[:, : rows - share, :] = total[...].reshape(parts, rows - share, width)
+
+
+def sum_kernel(in_ref, out_ref):
+    parts = in_ref.shape[0]
+    total = in_ref[0]
+    for d in range(1, parts):
+        total += in_ref[d]
+    out_ref[...] = jnp.broadcast_to(total[None], out_ref.shape)
 
 
 def middle_kernel(where_ref, g_ref, c_ref, a_ref, scaled_ref, message_ref, block):
@@ -123,28 +180,45 @@
     out_ref[...] = total[...].T.reshape(out_ref.shape)
 
 
-def combine_kernel(message_ref, chunk_ref, scale_ref):
+def combine_kernel(own_ref, message_ref, partial_ref, send_ref, keep_ref, chunk_ref, most_ref):
     senders, height, width = message_ref.shape
     piece = chunk_ref.shape[0]
-    all_most = message_ref[:, piece, :]
-    most = jnp.max(all_most, axis=0, keepdims=True)
-    scales = all_most / most
-    chunk = jnp.zeros(chunk_ref.shape, jnp.float32)
+    core = own_ref[1]
+    most = jnp.max(message_ref[:, piece, :], axis=0, keepdims=True)
+    chunk = jnp.zeros((piece, width), jnp.float32)
     for d in range(senders):
-        chunk += message_ref[d, :piece, :] * scales[d : d + 1, :]
+        chunk += message_ref[d, :piece, :] * (message_ref[d, piece : piece + 1, :] / most)
+    scale = message_ref[own_ref[0], piece : piece + 1, :] / most
+    halves = keep_ref.shape
+    send_ref[: send_ref.shape[0] - piece, :] = (partial_ref[:, 1 - core] * scale).reshape(
+        halves[0] * halves[1], width
+    )
+    send_ref[send_ref.shape[0] - piece :, :] = chunk
+    keep_ref[...] = partial_ref[:, core] * scale
     chunk_ref[...] = chunk
-    scale_ref[:senders, :] = scales
-    scale_ref[senders:, :] = jnp.broadcast_to(most, (scale_ref.shape[0] - senders, width))
-
-
-def last_kernel(parts_ref, h_ref, scale_ref, c_ref, out_ref):
-    senders, owned, width = parts_ref.shape
-    scales = scale_ref[:senders, :]
-    most = scale_ref[senders : senders + 1, :]
-    total = jnp.zeros((owned, width), jnp.float32)
-    for d in range(senders):
-        total += parts_ref[d] * scales[d : d + 1, :]
-    gram = h_ref[...].reshape(width, width)
+    most_ref[...] = jnp.broadcast_to(most, most_ref.shape)
+
+
+def pair_kernel(own_ref, keep_ref, chunk_ref, got_ref, out_ref, both):
+    targets, owned, width = keep_ref.shape
+    piece = chunk_ref.shape[0]
+    core = own_ref[1]
+    both[core] = chunk_ref[...]
+    both[1 - core] = got_ref[targets * owned :, :]
+    out_ref[:, :owned, :] = keep_ref[...] + got_ref[: targets * owned, :].reshape(keep_ref.shape)
+    out_ref[:, owned:, :] = jnp.broadcast_to(
+        both[...].reshape(1, 2 * piece, width), (targets, 2 * piece, width)
+    )
+
+
+def last_kernel(parts_ref, most_ref, c_ref, out_ref):
+    senders, height, width = parts_ref.shape
+    owned = out_ref.shape[0]
+    most = most_ref[:1, :]
+    total = parts_ref[0, :owned, :]
+    for d in range(1, senders):
+        total += parts_ref[d, :owned, :]
+    gram = parts_ref[:, owned:, :].reshape(width, width)
     same = lax.broadcasted_iota(jnp.int32, (width, width), 0) == lax.broadcasted_iota(
         jnp.int32, (width, width), 1
     )
@@ -156,91 +230,116 @@
     out_ref[...] = dot32(total * ratio, inverse(system))
 
 
+def limited(mebibytes):
+    return pltpu.CompilerParams(vmem_limit_bytes=mebibytes * 1024 * 1024)
+
+
 def per_device(tensor, factor_b, factor_c):
     slices, rows_block, cols_block = tensor.shape
     width = factor_c.shape[1]
     row_size = lax.axis_size(ROW)
     col_size = lax.axis_size(COL)
+    z_size = lax.axis_size("z")
     owned_a = rows_block // col_size
     owned_b = cols_block // row_size
     share_a = width // col_size
     share_b = width // row_size
     f32 = jnp.float32
-    params = pltpu.CompilerParams(vmem_limit_bytes=48 * 1024 * 1024)
-
-    b_block = lax.all_gather(factor_b, ROW, axis=0, tiled=True)
+    shape = jax.ShapeDtypeStruct
+
+    spread_b = jnp.broadcast_to(factor_b[None], (z_size,) + factor_b.shape)
+    mine = lax.all_to_all(spread_b, "z", 0, 0, tiled=True)
+    other = lax.ppermute(mine, "core", [(0, 1), (1, 0)])
+    core = lax.axis_index("core").astype(jnp.int32).reshape(1)
     packed = pl.pallas_call(
         first_kernel,
-        out_shape=jax.ShapeDtypeStruct((col_size, owned_a + share_a, width), f32),
-        in_specs=[ANY, VMEM, VMEM],
+        out_shape=shape((col_size, owned_a + share_a, width), f32),
+        in_specs=[SMEM, HBM, VMEM, VMEM, VMEM],
         out_specs=VMEM,
         scratch_shapes=[
-            pltpu.VMEM((slices, rows_block, cols_block), f32),
+            pltpu.VMEM(tensor.shape, f32),
+            pltpu.VMEM((z_size, 2, owned_b, width), f32),
             pltpu.VMEM((cols_block, 2 * width), jnp.bfloat16),
             pltpu.VMEM((rows_block, width), f32),
             pltpu.SemaphoreType.DMA((slices,)),
         ],
-        compiler_params=params,
+        compiler_params=limited(LARGE_MIB),
         name="first",
-    )(tensor, b_block, factor_c)
+    )(core, tensor, mine, other, factor_c)
     received = lax.all_to_all(packed, COL, 0, 0, tiled=True)
-    summed = jnp.sum(received, axis=0)
-    gathered = lax.all_to_all(
-        jnp.broadcast_to(summed[None], received.shape), COL, 0, 0, tiled=True
-    )
+    summed = pl.pallas_call(
+        sum_kernel,
+        out_shape=shape(received.shape, f32),
+        in_specs=[VMEM],
+        out_specs=VMEM,
+        compiler_params=limited(WORK_MIB),
+        name="sum",
+    )(received)
+    gathered = lax.all_to_all(summed, COL, 0, 0, tiled=True)
     where = lax.axis_index(COL).astype(jnp.int32).reshape(1)
     a_update, scaled, message = pl.pallas_call(
         middle_kernel,
         out_shape=(
-            jax.ShapeDtypeStruct((owned_a, width), f32),
-            jax.ShapeDtypeStruct((rows_block, width), f32),
-            jax.ShapeDtypeStruct((row_size, share_b + 8, width), f32),
+            shape((owned_a, width), f32),
+            shape((rows_block, width), f32),
+            shape((row_size, share_b + 8, width), f32),
         ),
         in_specs=[SMEM, VMEM, VMEM],
         out_specs=(VMEM, VMEM, VMEM),
         scratch_shapes=[pltpu.VMEM((rows_block, width), f32)],
+        compiler_params=limited(WORK_MIB),
         name="middle",
     )(where, gathered, factor_c)
     grams = lax.all_to_all(message, ROW, 0, 0, tiled=True)
     partial_b = pl.pallas_call(
         second_kernel,
-        out_shape=jax.ShapeDtypeStruct((row_size, owned_b, width), f32),
-        in_specs=[ANY, VMEM, VMEM],
+        out_shape=shape((row_size, owned_b, width), f32),
+        in_specs=[HBM, VMEM, VMEM],
         out_specs=VMEM,
         scratch_shapes=[
-            pltpu.VMEM((slices, rows_block, cols_block), f32),
+            pltpu.VMEM(tensor.shape, f32),
             pltpu.VMEM((width, cols_block), f32),
             pltpu.SemaphoreType.DMA((slices,)),
         ],
-        compiler_params=params,
+        compiler_params=limited(LARGE_MIB),
         cost_estimate=pl.CostEstimate(
-            flops=6 * slices * rows_block * cols_block * width,
-            bytes_accessed=4 * slices * rows_block * cols_block,
-            transcendentals=0,
+            flops=6 * tensor.size * width, bytes_accessed=4 * tensor.size, transcendentals=0
         ),
         name="second",
     )(tensor, scaled, factor_c)
-    chunk, scales = pl.pallas_call(
+    own = jnp.stack([lax.axis_index(ROW), lax.axis_index("core")]).astype(jnp.int32)
+    send, keep, chunk, most = pl.pallas_call(
         combine_kernel,
         out_shape=(
-            jax.ShapeDtypeStruct((share_b, width), f32),
-            jax.ShapeDtypeStruct((row_size + 8, width), f32),
+            shape((z_size * owned_b + share_b, width), f32),
+            shape((z_size, owned_b, width), f32),
+            shape((share_b, width), f32),
+            shape((8, width), f32),
         ),
-        in_specs=[VMEM],
-        out_specs=(VMEM, VMEM),
+        in_specs=[SMEM, VMEM, VMEM],
+        out_specs=(VMEM,) * 4,
+        compiler_params=limited(WORK_MIB),
         name="combine",
-    )(grams)
-    outgoing = jnp.concatenate(
-        [partial_b, jnp.broadcast_to(chunk[None], (row_size,) + chunk.shape)], axis=1
-    )
-    final = lax.all_to_all(outgoing, ROW, 0, 0, tiled=True)
+    )(own, grams, partial_b.reshape(z_size, 2, owned_b, width))
+    got = lax.ppermute(send, "core", [(0, 1), (1, 0)])
+    outgoing = pl.pallas_call(
+        pair_kernel,
+        out_shape=shape((z_size, owned_b + 2 * share_b, width), f32),
+        in_specs=[SMEM] + [VMEM] * 3,
+        out_specs=VMEM,
+        scratch_shapes=[pltpu.VMEM((2, share_b, width), f32)],
+        compiler_params=limited(WORK_MIB),
+        name="pair",
+    )(own, keep, chunk, got)
+    final = lax.all_to_all(outgoing, "z", 0, 0, tiled=True)
     b_update = pl.pallas_call(
         last_kernel,
-        out_shape=jax.ShapeDtypeStruct((owned_b, width), f32),
-        in_specs=[VMEM] * 4,
-        out_specs=VMEM,
+        out_shape=shape((owned_b, width), f32),
+        in_specs=[VMEM] * 3,
+        out_specs=VMEM,
+        compiler_params=limited(WORK_MIB),
         name="last",
-    )(final[:, :owned_b, :], final[:, owned_b:, :], scales, factor_c)
+    )(final, most, factor_c)
     return (a_update, b_update)
 
 

time: 123 us -> 99.7 us (0.81)
  Pallas kernels: 40.8 us -> 27.2 us
  blocking collectives: 54.2 us -> 43 us
  local copies, waits for them, and re-layouts: 5.8 us -> 1.44 us
  waiting for transfers between devices: 10.4 us -> 13.9 us
  starting transfers between devices: 10.4 us -> 12.8 us
    all_gather x1 -> x0, blocking collectives: 22.3 us -> none  [per_device(): b_block = lax.all_gather(factor_b, ROW, axis=0, tiled=True)]
    pallas_call x5 -> x7, Pallas kernels: 40.8 us -> 27.2 us  [the longest x1 7.46 us: per_device(): pl.pallas_call(middle_kernel, out_shape=(shape((owned_a, width), f32), sh...]
    all_to_all x1 -> x2, blocking collectives: 17.3 us -> 28.5 us  [the longest x1 16.6 us: per_device(): mine = lax.all_to_all(spread_b, 'z', 0, 0, tiled=True)]
    ppermute x0 -> x2, starting transfers between devices: none -> 2.39 us  [the longest x1 2.3 us: per_device(): other = lax.ppermute(mine, 'core', [(0, 1), (1, 0)])]
    ppermute x0 -> x2, waiting for transfers between devices: none -> 2.33 us  [the longest x1 1.34 us: per_device(): got = lax.ppermute(send, 'core', [(0, 1), (1, 0)])]
    unnamed x10 -> x4, local copies, waits for them, and re-layouts: 3.02 us -> 0.7 us
    slice x2 -> x0, local copies, waits for them, and re-layouts: 1.35 us -> none  [the longest x1 0.72 us: per_device(): final[:, :owned_b, :]]
  transfers between devices with their start and end apart: 2 -> 4, of which waited for: 2 -> 4; matrix products, arithmetic and copies ran while one was open for 0% -> 0% of each run, Pallas kernels for 4% -> 5%
where the time goes in v2:
time: 99.7 us; the launch traced here: 99.2 us
  blocking collectives  43 us (43%)
  Pallas kernels  27.2 us (27%)
  waiting for transfers between devices  13.9 us (14%)
  starting transfers between devices  12.8 us (13%)
  local copies, waits for them, and re-layouts  1.44 us (1%)
    all_to_all x1, blocking collectives, per_device(): mine = lax.all_to_all(spread_b, 'z', 0, 0, tiled=True)  16.6 us
    all_to_all x1, blocking collectives, per_device(): received = lax.all_to_all(packed, COL, 0, 0, tiled=True)  14.5 us
    all_to_all x1, blocking collectives, per_device(): final = lax.all_to_all(outgoing, 'z', 0, 0, tiled=True)  12 us
    all_to_all x1, waiting for transfers between devices, per_device(): gathered = lax.all_to_all(summed, COL, 0, 0, tiled=True)  7.66 us
    pallas_call x1, Pallas kernels, per_device(): pl.pallas_call(middle_kernel, out_shape=(shape((owned_a, width), f32), sh...  7.46 us
    pallas_call x1, Pallas kernels, per_device(): pl.pallas_call(first_kernel, out_shape=shape((col_size, owned_a + share_a...  6.72 us
    all_to_all x1, starting transfers between devices, per_device(): grams = lax.all_to_all(message, ROW, 0, 0, tiled=True)  6.41 us
    pallas_call x1, Pallas kernels, per_device(): pl.pallas_call(last_kernel, out_shape=shape((owned_b, width), f32), in_sp...  5.99 us
  transfers between devices with their start and end apart: 4, of which 4 were waited for; matrix products, arithmetic and copies ran while one was open for 0% of the time, Pallas kernels for 5%

profile of v2, /device:TPU:1, one launch (start us, length us, event | category | flops | bytes accessed | tf_op | source)
XLA Modules:
  0.0 99.2 jit_solution(13050020638157904781)
XLA Ops:
  0.6 0.0 copy-start.1
  0.6 0.7 broadcast_in_dim.2
  1.4 16.6 %all_to_all.25.mine_ref = f32[8,32,128]{2,1,0:T(8,128)S(1)} all-to-all(f32[8,32,128]{2,1,0:T(8,128)S(1)} %broadcast_in_dim.2), channel_id=1, replica_groups=mesh['z'=8,'core'=2,'x'=4,'y'=4] {'z'}, dimensions={0} | all-to-all | bytes 262144 | tf_op jit(solution)/shard_map/all_to_all | solution.py:251
  17.9 2.3 %collective-permute-start = (f32[8,32,128]{2,1,0:T(8,128)S(1)}, f32[8,32,128]{2,1,0:T(8,128)S(1)}, u32[]{:S(2)}, u32[]{:S(2)}) collective-permute-start(f32[8,32,128]{2,1,0:T(8,128)S(1)} %all_to_all.25.mine_ref), channel_id=1, source_target_pairs={{0,16},{16,0},{1,17},{17,1},{2,18},{18,2},{3,19},{19,3},{4,20},{20... | collective-permute-start | bytes 393224 | tf_op jit(solution)/shard_map/ppermute | solution.py:252
  20.2 1.0 collective-permute-done.other_ref
  21.2 0.0 copy-start
  21.2 0.7 copy-done
  21.9 6.7 %first.1 = f32[16,40,128]{2,1,0:T(8,128)S(1)} custom-call(s32[1]{0:T(128)} %bitcast.1.core_ref, f32[12,512,512]{2,1,0:T(8,128)} %t_hbm.3, f32[8,32,128]{2,1,0:T(8,128)S(1)} %all_to_all.25.mine_ref, f32[8,32,128]{2,1,0:T(8,128)S(1)} %collective-permute-done.other_ref, f32[12,128]{1,0:T(8,128)S(1)} %copy-done), custom_call_target="tpu_custom_call" | custom-call | tf_op jit(solution)/shard_map/first/pallas_call | solution.py:254
  28.6 14.5 %all_to_all.26.in_ref = f32[16,40,128]{2,1,0:T(8,128)S(1)} all-to-all(f32[16,40,128]{2,1,0:T(8,128)S(1)} %first.1), channel_id=1, replica_groups=mesh['z'=8,'core'=2,'x'=4,'y'=4] {'x','y'}, dimensions={0} | all-to-all | bytes 655360 | tf_op jit(solution)/shard_map/all_to_all | solution.py:269
  43.1 0.8 sum.1
  43.9 4.0 %all-to-all-start.2 = ((f32[16,40,128]{2,1,0:T(8,128)}), f32[16,40,128]{2,1,0:T(8,128)S(1)}, u32[]{:S(2)}, u32[]{:S(2)}) async-start(f32[16,40,128]{2,1,0:T(8,128)} %sum.1), calls=%async_computation.2 | async-start | bytes 655360 | tf_op jit(solution)/shard_map/all_to_all | solution.py:278
  48.0 7.7 %all-to-all-done.2.g_ref = f32[16,40,128]{2,1,0:T(8,128)S(1)} async-done(((f32[16,40,128]{2,1,0:T(8,128)}), f32[16,40,128]{2,1,0:T(8,128)S(1)}, u32[]{:S(2)}, u32[]{:S(2)}) %all-to-all-start.2) | async-done | bytes 327712 | tf_op jit(solution)/shard_map/all_to_all | solution.py:278
  55.6 0.0 copy-done.1
  55.6 7.5 %middle.1 = (f32[32,128]{1,0:T(8,128)}, f32[512,128]{1,0:T(8,128)S(1)}, f32[16,16,128]{2,1,0:T(8,128)}) custom-call(s32[1]{0:T(128)} %bitcast.where_ref, f32[16,40,128]{2,1,0:T(8,128)S(1)} %all-to-all-done.2.g_ref, f32[12,128]{1,0:T(8,128)S(1)} %copy-done.1), custom_call_target="tpu_custom_call" | custom-call | tf_op jit(solution)/shard_map/middle/pallas_call | solution.py:280
  63.1 6.4 %all-to-all-start.3 = ((f32[16,16,128]{2,1,0:T(8,128)}), f32[16,16,128]{2,1,0:T(8,128)S(1)}, u32[]{:S(2)}, u32[]{:S(2)}) async-start(f32[16,16,128]{2,1,0:T(8,128)} %get-tuple-element.10), calls=%async_computation.3 | async-start | bytes 262144 | tf_op jit(solution)/shard_map/all_to_all | solution.py:293
  69.5 0.1 pad_add_fusion.own_ref
  69.6 5.2 %second.1 = f32[16,32,128]{2,1,0:T(8,128)S(1)} custom-call(f32[12,512,512]{2,1,0:T(8,128)} %t_hbm.3, f32[512,128]{1,0:T(8,128)S(1)} %get-tuple-element.11.scaled_ref, f32[12,128]{1,0:T(8,128)S(1)} %copy-done.1), custom_call_target="tpu_custom_call" | custom-call | flops 2415919104 | bytes 12582912 | tf_op jit(solution)/shard_map/second/pallas_call | solution.py:294
  74.8 3.9 %all-to-all-done.3.message_ref = f32[16,16,128]{2,1,0:T(8,128)S(1)} async-done(((f32[16,16,128]{2,1,0:T(8,128)}), f32[16,16,128]{2,1,0:T(8,128)S(1)}, u32[]{:S(2)}, u32[]{:S(2)}) %all-to-all-start.3) | async-done | bytes 131104 | tf_op jit(solution)/shard_map/all_to_all | solution.py:293
  78.7 0.6 combine.1
  79.3 0.1 collective-permute-start.1
  79.4 1.3 %collective-permute-done.1.got_ref = f32[264,128]{1,0:T(8,128)S(1)} collective-permute-done((f32[264,128]{1,0:T(8,128)S(1)}, f32[264,128]{1,0:T(8,128)S(1)}, u32[]{:S(2)}, u32[]{:S(2)}) %collective-permute-start.1) | collective-permute-done | bytes 135200 | tf_op jit(solution)/shard_map/ppermute | solution.py:324
  80.7 0.6 pair.1
  81.3 12.0 %all_to_all.27.parts_ref = f32[8,48,128]{2,1,0:T(8,128)S(1)} all-to-all(f32[8,48,128]{2,1,0:T(8,128)S(1)} %pair.1), channel_id=1, replica_groups=mesh['z'=8,'core'=2,'x'=4,'y'=4] {'z'}, dimensions={0} | all-to-all | bytes 393216 | tf_op jit(solution)/shard_map/all_to_all | solution.py:334
  93.2 6.0 %last.1 = f32[32,128]{1,0:T(8,128)} custom-call(f32[8,48,128]{2,1,0:T(8,128)S(1)} %all_to_all.27.parts_ref, f32[8,128]{1,0:T(8,128)S(1)} %get-tuple-element.15.most_ref, f32[12,128]{1,0:T(8,128)S(1)} %copy-done.1), custom_call_target="tpu_custom_call" | custom-call | tf_op jit(solution)/shard_map/last/pallas_call | solution.py:335
Async XLA Ops:
  0.6 55.0 %copy-start.1 = (f32[12,128]{1,0:T(8,128)S(1)}, f32[12,128]{1,0:T(8,128)}, u32[]{:S(2)}) copy-start(f32[12,128]{1,0:T(8,128)} %c_ref.7) | copy-start | bytes 18436
  17.9 3.3 %collective-permute-start = (f32[8,32,128]{2,1,0:T(8,128)S(1)}, f32[8,32,128]{2,1,0:T(8,128)S(1)}, u32[]{:S(2)}, u32[]{:S(2)}) collective-permute-start(f32[8,32,128]{2,1,0:T(8,128)S(1)} %all_to_all.25.mine_ref), channel_id=1, source_target_pairs={{0,16},{16,0},{1,17},{17,1},{2,18},{18,2},{3,19},{19,3},{4,20},{20... | collective-permute-start | bytes 393224 | tf_op jit(solution)/shard_map/ppermute | solution.py:252
  21.2 0.7 copy-start
  43.9 11.7 %all-to-all-start.2 = ((f32[16,40,128]{2,1,0:T(8,128)}), f32[16,40,128]{2,1,0:T(8,128)S(1)}, u32[]{:S(2)}, u32[]{:S(2)}) async-start(f32[16,40,128]{2,1,0:T(8,128)} %sum.1), calls=%async_computation.2 | async-start | bytes 655360 | tf_op jit(solution)/shard_map/all_to_all | solution.py:278
  63.1 15.6 %all-to-all-start.3 = ((f32[16,16,128]{2,1,0:T(8,128)}), f32[16,16,128]{2,1,0:T(8,128)S(1)}, u32[]{:S(2)}, u32[]{:S(2)}) async-start(f32[16,16,128]{2,1,0:T(8,128)} %get-tuple-element.10), calls=%async_computation.3 | async-start | bytes 262144 | tf_op jit(solution)/shard_map/all_to_all | solution.py:293
  79.3 1.4 %collective-permute-start.1 = (f32[264,128]{1,0:T(8,128)S(1)}, f32[264,128]{1,0:T(8,128)S(1)}, u32[]{:S(2)}, u32[]{:S(2)}) collective-permute-start(f32[264,128]{1,0:T(8,128)S(1)} %get-tuple-element.14), channel_id=1, source_target_pairs={{0,16},{16,0},{1,17},{17,1},{2,18},{18,2},{3,19},{19,3},{4,20},{20... | collective-permute-start | bytes 405512 | tf_op jit(solution)/shard_map/ppermute | solution.py:324

commit v3 on v2

--- a/solution.py
+++ b/solution.py
@@ -1,3 +1,5 @@
+import functools
+
 import jax
 import jax.numpy as jnp
 from jax import lax
@@ -6,6 +8,7 @@
 from jax.sharding import Mesh
 from jax.sharding import PartitionSpec as P
 
+
 EPSILON = 1e-06
 HIGHEST = lax.Precision.HIGHEST
 VMEM = pl.BlockSpec(memory_space=pltpu.VMEM)
@@ -13,6 +16,8 @@
 SMEM = pl.BlockSpec(memory_space=pltpu.SMEM)
 ROW = ("z", "core")
 COL = ("x", "y")
+TINY = 1e-30
+PARTS = 3
 LARGE_MIB = 52
 WORK_MIB = 12
 
@@ -97,8 +102,9 @@
     return jnp.concatenate(strips, axis=0)
 
 
-def first_kernel(core_ref, t_hbm, mine_ref, other_ref, c_ref, out_ref, t_buf, b_block, b_both, total, sems):
+def first_kernel(core_ref, t_hbm, mine_ref, other_ref, c_hbm, out_ref, t_buf, b_block, b_both, total, c_ref, sems):
     slices = t_hbm.shape[0]
+    pltpu.make_async_copy(c_hbm, c_ref, sems.at[slices]).start()
     for k in range(slices):
         pltpu.make_async_copy(t_hbm.at[k], t_buf.at[k], sems.at[k]).start()
     core = core_ref[0]
@@ -113,6 +119,7 @@
     parts, rows, _ = out_ref.shape
     share = width // parts
     out_ref[:, rows - share :, :] = gram.reshape(parts, share, width)
+    pltpu.make_async_copy(c_hbm, c_ref, sems.at[slices]).wait()
     for k in range(slices):
         pltpu.make_async_copy(t_hbm.at[k], t_buf.at[k], sems.at[k]).wait()
         t_high, t_low = split(t_buf[k])
@@ -146,88 +153,100 @@
     start = pl.multiple_of(where_ref[0] * owned, owned)
     a_ref[...] = block[pl.ds(start, owned), :]
     most = jnp.max(jnp.abs(update), axis=0, keepdims=True)
-    most = jnp.where(most > 0.0, most, 1.0)
+    most = jnp.where(most > 0.0, most, TINY)
     scaled = update / most
     scaled_ref[...] = scaled
-    gram = contract_rows(update, scaled)
-    targets, height, _ = message_ref.shape
-    piece = width // targets
-    message_ref[:, :piece, :] = gram.reshape(targets, piece, width)
-    message_ref[:, piece:, :] = jnp.broadcast_to(
-        most.reshape(1, 1, width), (targets, height - piece, width)
-    )
-
-
-def second_kernel(t_hbm, scaled_ref, c_ref, out_ref, t_buf, total, sems):
-    slices = t_hbm.shape[0]
+    message_ref[:width, :] = contract_rows(update, scaled)
+    message_ref[width:, :] = jnp.broadcast_to(most, (message_ref.shape[0] - width, width))
+
+
+def merge(mine_ref, got_ref):
+    width = mine_ref.shape[1]
+    mine = mine_ref[width : width + 1, :]
+    got = got_ref[width : width + 1, :]
+    most = jnp.maximum(mine, got)
+    return mine_ref[:width, :] * (mine / most) + got_ref[:width, :] * (got / most), most
+
+
+def merge_kernel(mine_ref, got_ref, out_ref):
+    gram, most = merge(mine_ref, got_ref)
+    width = gram.shape[1]
+    out_ref[:width, :] = gram
+    out_ref[width:, :] = jnp.broadcast_to(most, (out_ref.shape[0] - width, width))
+
+
+def partial_sum(begin, t_hbm, scaled_ref, c_ref, total, t_buf, sems, fresh):
+    slices = t_buf.shape[0]
     for k in range(slices):
-        pltpu.make_async_copy(t_hbm.at[k], t_buf.at[k], sems.at[k]).start()
+        pltpu.make_async_copy(t_hbm.at[begin + k], t_buf.at[k], sems.at[k]).start()
     turned = scaled_ref[...].T
     width = turned.shape[0]
     c_turned = c_ref[...].T
     for k in range(slices):
-        w_high, w_low = split(turned * c_turned[:, k : k + 1])
+        w_high, w_low = split(turned * c_turned[:, begin + k : begin + k + 1])
         w_both = jnp.concatenate([w_high, w_low], axis=0)
-        pltpu.make_async_copy(t_hbm.at[k], t_buf.at[k], sems.at[k]).wait()
+        pltpu.make_async_copy(t_hbm.at[begin + k], t_buf.at[k], sems.at[k]).wait()
         t_high, t_low = split(t_buf[k])
         main = jnp.dot(w_both, t_high, preferred_element_type=jnp.float32)
         rest = jnp.dot(w_high, t_low, preferred_element_type=jnp.float32)
         term = main[:width] + (main[width:] + rest)
-        if k == 0:
+        if fresh and k == 0:
             total[...] = term
         else:
             total[...] += term
-    out_ref[...] = total[...].T.reshape(out_ref.shape)
-
-
-def combine_kernel(own_ref, message_ref, partial_ref, send_ref, keep_ref, chunk_ref, most_ref):
-    senders, height, width = message_ref.shape
-    piece = chunk_ref.shape[0]
-    core = own_ref[1]
-    most = jnp.max(message_ref[:, piece, :], axis=0, keepdims=True)
-    chunk = jnp.zeros((piece, width), jnp.float32)
-    for d in range(senders):
-        chunk += message_ref[d, :piece, :] * (message_ref[d, piece : piece + 1, :] / most)
-    scale = message_ref[own_ref[0], piece : piece + 1, :] / most
-    halves = keep_ref.shape
-    send_ref[: send_ref.shape[0] - piece, :] = (partial_ref[:, 1 - core] * scale).reshape(
-        halves[0] * halves[1], width
-    )
-    send_ref[send_ref.shape[0] - piece :, :] = chunk
-    keep_ref[...] = partial_ref[:, core] * scale
-    chunk_ref[...] = chunk
-    most_ref[...] = jnp.broadcast_to(most, most_ref.shape)
-
-
-def pair_kernel(own_ref, keep_ref, chunk_ref, got_ref, out_ref, both):
+
+
+def head_kernel(begin, t_hbm, scaled_ref, c_ref, out_ref, t_buf, sems):
+    partial_sum(begin, t_hbm, scaled_ref, c_ref, out_ref, t_buf, sems, True)
+
+
+def body_kernel(begin, t_hbm, scaled_ref, c_ref, in_ref, out_ref, t_buf, sems):
+    out_ref[...] = in_ref[...]
+    partial_sum(begin, t_hbm, scaled_ref, c_ref, out_ref, t_buf, sems, False)
+
+
+def tail_kernel(begin, core_ref, t_hbm, scaled_ref, c_ref, in_ref, message_ref, pair_ref, send_ref, keep_ref, total, halves, t_buf, sems):
+    total[...] = in_ref[...]
+    partial_sum(begin, t_hbm, scaled_ref, c_ref, total, t_buf, sems, False)
+    width = scaled_ref.shape[1]
+    scale = message_ref[width : width + 1, :] / pair_ref[width : width + 1, :]
+    halves[...] = (total[...].T * scale).reshape(halves.shape)
+    core = core_ref[0]
+    send_ref[...] = halves[:, 1 - core].reshape(send_ref.shape)
+    keep_ref[...] = halves[:, core]
+
+
+def pair_kernel(keep_ref, got_ref, pair_ref, out_ref):
     targets, owned, width = keep_ref.shape
-    piece = chunk_ref.shape[0]
-    core = own_ref[1]
-    both[core] = chunk_ref[...]
-    both[1 - core] = got_ref[targets * owned :, :]
-    out_ref[:, :owned, :] = keep_ref[...] + got_ref[: targets * owned, :].reshape(keep_ref.shape)
+    out_ref[:, :owned, :] = keep_ref[...] + got_ref[...].reshape(keep_ref.shape)
     out_ref[:, owned:, :] = jnp.broadcast_to(
-        both[...].reshape(1, 2 * piece, width), (targets, 2 * piece, width)
-    )
-
-
-def last_kernel(parts_ref, most_ref, c_ref, out_ref):
-    senders, height, width = parts_ref.shape
-    owned = out_ref.shape[0]
-    most = most_ref[:1, :]
-    total = parts_ref[0, :owned, :]
-    for d in range(1, senders):
-        total += parts_ref[d, :owned, :]
-    gram = parts_ref[:, owned:, :].reshape(width, width)
+        pair_ref[width : width + 1, :].reshape(1, 1, width),
+        (targets, out_ref.shape[1] - owned, width),
+    )
+
+
+def solve_kernel(mine_ref, got_ref, c_ref, out_ref):
+    gram, most = merge(mine_ref, got_ref)
+    width = gram.shape[1]
     same = lax.broadcasted_iota(jnp.int32, (width, width), 0) == lax.broadcasted_iota(
         jnp.int32, (width, width), 1
     )
     norms = jnp.sqrt(jnp.sum(jnp.where(same, gram, 0.0), axis=0, keepdims=True) * most + EPSILON)
-    ratio = most / norms
     flipped = jnp.sum(jnp.where(same, jnp.broadcast_to(norms, (width, width)), 0.0), axis=1, keepdims=True)
     factor_c = c_ref[...]
-    system = contract_rows(factor_c, factor_c) * ((gram * ratio) / flipped)
-    out_ref[...] = dot32(total * ratio, inverse(system))
+    system = contract_rows(factor_c, factor_c) * ((gram * (most / norms)) / flipped)
+    out_ref[:width, :] = inverse(system)
+    out_ref[width:, :] = jnp.broadcast_to(norms, (out_ref.shape[0] - width, width))
+
+
+def last_kernel(parts_ref, solved_ref, out_ref):
+    senders, _, width = parts_ref.shape
+    owned = out_ref.shape[0]
+    norms = solved_ref[width : width + 1, :]
+    total = jnp.zeros((owned, width), jnp.float32)
+    for d in range(senders):
+        total += parts_ref[d, :owned, :] * (parts_ref[d, owned : owned + 1, :] / norms)
+    out_ref[...] = dot32(total, solved_ref[:width, :])
 
 
 def limited(mebibytes):
@@ -243,7 +262,6 @@
     owned_a = rows_block // col_size
     owned_b = cols_block // row_size
     share_a = width // col_size
-    share_b = width // row_size
     f32 = jnp.float32
     shape = jax.ShapeDtypeStruct
 
@@ -254,14 +272,15 @@
     packed = pl.pallas_call(
         first_kernel,
         out_shape=shape((col_size, owned_a + share_a, width), f32),
-        in_specs=[SMEM, HBM, VMEM, VMEM, VMEM],
+        in_specs=[SMEM, HBM, VMEM, VMEM, HBM],
         out_specs=VMEM,
         scratch_shapes=[
             pltpu.VMEM(tensor.shape, f32),
             pltpu.VMEM((z_size, 2, owned_b, width), f32),
             pltpu.VMEM((cols_block, 2 * width), jnp.bfloat16),
             pltpu.VMEM((rows_block, width), f32),
-            pltpu.SemaphoreType.DMA((slices,)),
+            pltpu.VMEM(factor_c.shape, f32),
+            pltpu.SemaphoreType.DMA((slices + 1,)),
         ],
         compiler_params=limited(LARGE_MIB),
         name="first",
@@ -282,7 +301,7 @@
         out_shape=(
             shape((owned_a, width), f32),
             shape((rows_block, width), f32),
-            shape((row_size, share_b + 8, width), f32),
+            shape((width + 8, width), f32),
         ),
         in_specs=[SMEM, VMEM, VMEM],
         out_specs=(VMEM, VMEM, VMEM),
@@ -290,62 +309,111 @@
         compiler_params=limited(WORK_MIB),
         name="middle",
     )(where, gathered, factor_c)
-    grams = lax.all_to_all(message, ROW, 0, 0, tiled=True)
-    partial_b = pl.pallas_call(
-        second_kernel,
-        out_shape=shape((row_size, owned_b, width), f32),
+    small = limited(WORK_MIB)
+    swap = [(0, 1), (1, 0)]
+    per_part = slices // PARTS
+    part_cost = pl.CostEstimate(
+        flops=6 * tensor.size * width // PARTS,
+        bytes_accessed=4 * tensor.size // PARTS,
+        transcendentals=0,
+    )
+    part_scratch = [
+        pltpu.VMEM((per_part, rows_block, cols_block), f32),
+        pltpu.SemaphoreType.DMA((per_part,)),
+    ]
+    running = shape((width, cols_block), f32)
+
+    def merged(mine, got):
+        return pl.pallas_call(
+            merge_kernel,
+            out_shape=shape(message.shape, f32),
+            in_specs=[VMEM, VMEM],
+            out_specs=VMEM,
+            compiler_params=small,
+            name="merge",
+        )(mine, got)
+
+    def flipped(array, distance):
+        return lax.ppermute(array, "z", [(i, i ^ distance) for i in range(z_size)])
+
+    got = lax.ppermute(message, "core", swap)
+    total = pl.pallas_call(
+        functools.partial(head_kernel, 0),
+        out_shape=running,
         in_specs=[HBM, VMEM, VMEM],
         out_specs=VMEM,
+        scratch_shapes=part_scratch,
+        compiler_params=limited(LARGE_MIB),
+        cost_estimate=part_cost,
+        name="head",
+    )(tensor, scaled, factor_c)
+    pair = merged(message, got)
+    got = flipped(pair, 1)
+    total = pl.pallas_call(
+        functools.partial(body_kernel, per_part),
+        out_shape=running,
+        in_specs=[HBM, VMEM, VMEM, VMEM],
+        out_specs=VMEM,
+        scratch_shapes=part_scratch,
+        compiler_params=limited(LARGE_MIB),
+        cost_estimate=part_cost,
+        name="body",
+    )(tensor, scaled, factor_c, total)
+    quad = merged(pair, got)
+    got = flipped(quad, 2)
+    send, keep = pl.pallas_call(
+        functools.partial(tail_kernel, 2 * per_part),
+        out_shape=(
+            shape((z_size * owned_b, width), f32),
+            shape((z_size, owned_b, width), f32),
+        ),
+        in_specs=[SMEM, HBM] + [VMEM] * 5,
+        out_specs=(VMEM, VMEM),
         scratch_shapes=[
-            pltpu.VMEM(tensor.shape, f32),
             pltpu.VMEM((width, cols_block), f32),
-            pltpu.SemaphoreType.DMA((slices,)),
-        ],
+            pltpu.VMEM((z_size, 2, owned_b, width), f32),
+        ]
+        + part_scratch,
         compiler_params=limited(LARGE_MIB),
-        cost_estimate=pl.CostEstimate(
-            flops=6 * tensor.size * width, bytes_accessed=4 * tensor.size, transcendentals=0
-        ),
-        name="second",
-    )(tensor, scaled, factor_c)
-    own = jnp.stack([lax.axis_index(ROW), lax.axis_index("core")]).astype(jnp.int32)
-    send, keep, chunk, most = pl.pallas_call(
-        combine_kernel,
-        out_shape=(
-            shape((z_size * owned_b + share_b, width), f32),
-            shape((z_size, owned_b, width), f32),
-            shape((share_b, width), f32),
-            shape((8, width), f32),
-        ),
-        in_specs=[SMEM, VMEM, VMEM],
-        out_specs=(VMEM,) * 4,
-        compiler_params=limited(WORK_MIB),
-        name="combine",
-    )(own, grams, partial_b.reshape(z_size, 2, owned_b, width))
-    got = lax.ppermute(send, "core", [(0, 1), (1, 0)])
+        cost_estimate=part_cost,
+        name="tail",
+    )(core, tensor, scaled, factor_c, total, message, pair)
+    octet = merged(quad, got)
+    other_half = lax.ppermute(send, "core", swap)
+    got = flipped(octet, 4)
     outgoing = pl.pallas_call(
         pair_kernel,
-        out_shape=shape((z_size, owned_b + 2 * share_b, width), f32),
-        in_specs=[SMEM] + [VMEM] * 3,
-        out_specs=VMEM,
-        scratch_shapes=[pltpu.VMEM((2, share_b, width), f32)],
-        compiler_params=limited(WORK_MIB),
+        out_shape=shape((z_size, owned_b + 8, width), f32),
+        in_specs=[VMEM] * 3,
+        out_specs=VMEM,
+        compiler_params=small,
         name="pair",
-    )(own, keep, chunk, got)
+    )(keep, other_half, pair)
     final = lax.all_to_all(outgoing, "z", 0, 0, tiled=True)
+    solved = pl.pallas_call(
+        solve_kernel,
+        out_shape=shape(message.shape, f32),
+        in_specs=[VMEM] * 3,
+        out_specs=VMEM,
+        compiler_params=small,
+        cost_estimate=pl.CostEstimate(flops=10**9, bytes_accessed=10**6, transcendentals=0),
+        name="solve",
+    )(octet, got, factor_c)
     b_update = pl.pallas_call(
         last_kernel,
         out_shape=shape((owned_b, width), f32),
-        in_specs=[VMEM] * 3,
-        out_specs=VMEM,
-        compiler_params=limited(WORK_MIB),
+        in_specs=[VMEM, VMEM],
+        out_specs=VMEM,
+        compiler_params=small,
         name="last",
-    )(final, most, factor_c)
+    )(final, solved)
     return (a_update, b_update)
 
 
 def solution(mesh):
     finer = Mesh(mesh.devices.reshape(8, 2, 4, 4), ("z", "core", "x", "y"))
     placed = (P(None, ROW, COL), P(COL + ROW, None), P())
+
     return jax.shard_map(
         per_device,
         mesh=finer,

time: 99.7 us -> 102 us (1.023)
  blocking collectives: 43 us -> 31.1 us
  starting transfers between devices: 12.8 us -> 19.8 us
  waiting for transfers between devices: 13.9 us -> 19.5 us
  Pallas kernels: 27.2 us -> 28.8 us
    all_to_all x1 -> x0, blocking collectives: 12 us -> none  [per_device(): final = lax.all_to_all(outgoing, 'z', 0, 0, tiled=True)]
    ppermute x1 -> x5, starting transfers between devices: 0.09 us -> 10.1 us  [the longest x3 6.95 us: flipped(): return lax.ppermute(array, 'z', [(i, i ^ distance) for i in range(z_size)])]
    ppermute x1 -> x5, waiting for transfers between devices: 1.34 us -> 10.9 us  [the longest x3 9.71 us: flipped(): return lax.ppermute(array, 'z', [(i, i ^ distance) for i in range(z_size)])]
    pallas_call x3 -> x8, Pallas kernels: 6.33 us -> 13.7 us  [the longest x1 5.04 us: per_device(): pl.pallas_call(solve_kernel, out_shape=shape(message.shape, f32), in_spec...]
    pallas_call x1, Pallas kernels: 5.99 us -> 0.78 us  [per_device(): pl.pallas_call(last_kernel, out_shape=shape((owned_b, width), f32), in_sp...]
    all_to_all x1, waiting for transfers between devices: 3.91 us -> 0.01 us  [per_device(): final = lax.all_to_all(outgoing, 'z', 0, 0, tiled=True)]
    all_to_all x1, starting transfers between devices: 6.41 us -> 3.38 us  [per_device(): final = lax.all_to_all(outgoing, 'z', 0, 0, tiled=True)]
  transfers between devices with their start and end apart: 4 -> 8, of which waited for: 4 -> 5; matrix products, arithmetic and copies ran while one was open for 0% -> 0% of each run, Pallas kernels for 5% -> 8%
where the time goes in v3:
time: 102 us; the launch traced here: 101 us
  blocking collectives  31.1 us (30%)
  Pallas kernels  28.8 us (28%)
  starting transfers between devices  19.8 us (19%)
  waiting for transfers between devices  19.5 us (19%)
  local copies, waits for them, and re-layouts  1.44 us (1%)
    all_to_all x1, blocking collectives, per_device(): mine = lax.all_to_all(spread_b, 'z', 0, 0, tiled=True)  16.6 us
    all_to_all x1, blocking collectives, per_device(): received = lax.all_to_all(packed, COL, 0, 0, tiled=True)  14.5 us
    ppermute x3, waiting for transfers between devices, flipped(): return lax.ppermute(array, 'z', [(i, i ^ distance) for i in range(z_size)])  9.71 us
    all_to_all x1, waiting for transfers between devices, per_device(): gathered = lax.all_to_all(summed, COL, 0, 0, tiled=True)  7.66 us
    ppermute x3, starting transfers between devices, flipped(): return lax.ppermute(array, 'z', [(i, i ^ distance) for i in range(z_size)])  6.95 us
    pallas_call x1, Pallas kernels, per_device(): pl.pallas_call(middle_kernel, out_shape=(shape((owned_a, width), f32), sh...  6.88 us
    pallas_call x1, Pallas kernels, per_device(): pl.pallas_call(first_kernel, out_shape=shape((col_size, owned_a + share_a...  6.73 us
    pallas_call x1, Pallas kernels, per_device(): pl.pallas_call(solve_kernel, out_shape=shape(message.shape, f32), in_spec...  5.04 us
  transfers between devices with their start and end apart: 8, of which 5 were waited for; matrix products, arithmetic and copies ran while one was open for 0% of the time, Pallas kernels for 8%

profile of v3, /device:TPU:1, one launch (start us, length us, event | category | flops | bytes accessed | tf_op | source)
XLA Modules:
  0.0 101.4 jit_solution(1691326513722517640)
XLA Ops:
  0.6 0.7 broadcast_in_dim.2
  1.4 16.6 %all_to_all.20.mine_ref = f32[8,32,128]{2,1,0:T(8,128)S(1)} all-to-all(f32[8,32,128]{2,1,0:T(8,128)S(1)} %broadcast_in_dim.2), channel_id=1, replica_groups=mesh['z'=8,'core'=2,'x'=4,'y'=4] {'z'}, dimensions={0} | all-to-all | bytes 262144 | tf_op jit(solution)/shard_map/all_to_all | solution.py:269
  17.9 2.3 %collective-permute-start = (f32[8,32,128]{2,1,0:T(8,128)S(1)}, f32[8,32,128]{2,1,0:T(8,128)S(1)}, u32[]{:S(2)}, u32[]{:S(2)}) collective-permute-start(f32[8,32,128]{2,1,0:T(8,128)S(1)} %all_to_all.20.mine_ref), channel_id=1, source_target_pairs={{0,16},{16,0},{1,17},{17,1},{2,18},{18,2},{3,19},{19,3},{4,20},{20... | collective-permute-start | bytes 393224 | tf_op jit(solution)/shard_map/ppermute | solution.py:270
  20.2 1.0 collective-permute-done.other_ref
  21.2 0.7 copy-done
  21.9 6.7 %first.1 = f32[16,40,128]{2,1,0:T(8,128)S(1)} custom-call(s32[1]{0:T(128)} %bitcast.1.core_ref, f32[12,512,512]{2,1,0:T(8,128)} %t_hbm.7, f32[8,32,128]{2,1,0:T(8,128)S(1)} %all_to_all.20.mine_ref, f32[8,32,128]{2,1,0:T(8,128)S(1)} %collective-permute-done.other_ref, f32[12,128]{1,0:T(8,128)S(1)} %copy-done), custom_call_target="tpu_custom_call" | custom-call | tf_op jit(solution)/shard_map/first/pallas_call | solution.py:272
  28.6 14.5 %all_to_all.21.in_ref = f32[16,40,128]{2,1,0:T(8,128)S(1)} all-to-all(f32[16,40,128]{2,1,0:T(8,128)S(1)} %first.1), channel_id=1, replica_groups=mesh['z'=8,'core'=2,'x'=4,'y'=4] {'x','y'}, dimensions={0} | all-to-all | bytes 655360 | tf_op jit(solution)/shard_map/all_to_all | solution.py:288
  43.2 0.8 sum.1
  43.9 4.1 %all-to-all-start.2 = ((f32[16,40,128]{2,1,0:T(8,128)}), f32[16,40,128]{2,1,0:T(8,128)S(1)}, u32[]{:S(2)}, u32[]{:S(2)}) async-start(f32[16,40,128]{2,1,0:T(8,128)} %sum.1), calls=%async_computation.2 | async-start | bytes 655360 | tf_op jit(solution)/shard_map/all_to_all | solution.py:297
  48.0 7.7 %all-to-all-done.2.g_ref = f32[16,40,128]{2,1,0:T(8,128)S(1)} async-done(((f32[16,40,128]{2,1,0:T(8,128)}), f32[16,40,128]{2,1,0:T(8,128)S(1)}, u32[]{:S(2)}, u32[]{:S(2)}) %all-to-all-start.2) | async-done | bytes 327712 | tf_op jit(solution)/shard_map/all_to_all | solution.py:297
  55.6 6.9 %middle.1 = (f32[32,128]{1,0:T(8,128)}, f32[512,128]{1,0:T(8,128)S(1)}, f32[136,128]{1,0:T(8,128)S(1)}) custom-call(s32[1]{0:T(128)} %bitcast.where_ref, f32[16,40,128]{2,1,0:T(8,128)S(1)} %all-to-all-done.2.g_ref, f32[12,128]{1,0:T(8,128)S(1)} %copy-done.1), custom_call_target="tpu_custom_call" | custom-call | tf_op jit(solution)/shard_map/middle/pallas_call | solution.py:299
  62.5 2.6 %head.1.in_ref = f32[128,512]{1,0:T(8,128)S(1)} custom-call(f32[12,512,512]{2,1,0:T(8,128)} %t_hbm.7, f32[512,128]{1,0:T(8,128)S(1)} %get-tuple-element.8.scaled_ref, f32[12,128]{1,0:T(8,128)S(1)} %copy-done.1), custom_call_target="tpu_custom_call" | custom-call | flops 805306368 | bytes 4194304 | tf_op jit(solution)/shard_map/head/pallas_call | solution.py:340
  65.1 3.0 %collective-permute-start.1 = (f32[136,128]{1,0:T(8,128)S(1)}, f32[136,128]{1,0:T(8,128)S(1)}, u32[]{:S(2)}, u32[]{:S(2)}) collective-permute-start(f32[136,128]{1,0:T(8,128)S(1)} %get-tuple-element.9.mine_ref.message_ref), channel_id=1, source_target_pairs={{0,16},{16,0},{1,17},{17,1},{2,18},{18,2},{3,19},{19,3},{4,20},{20... | collective-permute-start | bytes 208904 | tf_op jit(solution)/shard_map/ppermute | solution.py:339
  68.1 2.6 %body.1.in_ref = f32[128,512]{1,0:T(8,128)S(1)} custom-call(f32[12,512,512]{2,1,0:T(8,128)} %t_hbm.7, f32[512,128]{1,0:T(8,128)S(1)} %get-tuple-element.8.scaled_ref, f32[12,128]{1,0:T(8,128)S(1)} %copy-done.1, f32[128,512]{1,0:T(8,128)S(1)} %head.1.in_ref), custom_call_target="tpu_custom_call" | custom-call | flops 805306368 | bytes 4194304 | tf_op jit(solution)/shard_map/body/pallas_call | solution.py:352
  70.8 2.7 %tail.1 = (f32[256,128]{1,0:T(8,128)S(1)}, f32[8,32,128]{2,1,0:T(8,128)S(1)}) custom-call(s32[1]{0:T(128)} %bitcast.1.core_ref, f32[12,512,512]{2,1,0:T(8,128)} %t_hbm.7, f32[512,128]{1,0:T(8,128)S(1)} %get-tuple-element.8.scaled_ref, f32[12,128]{1,0:T(8,128)S(1)} %copy-done.1, f32[128,512]{1,0:T(8,128)S(1)} %body.1.in_ref, ...), custom_call_target="tpu_custom_call" | custom-call | flops 805306368 | bytes 4194304 | tf_op jit(solution)/shard_map/tail/pallas_call | solution.py:364
  73.8 1.1 %collective-permute-done.2.got_ref = f32[256,128]{1,0:T(8,128)S(1)} collective-permute-done((f32[256,128]{1,0:T(8,128)S(1)}, f32[256,128]{1,0:T(8,128)S(1)}, u32[]{:S(2)}, u32[]{:S(2)}) %collective-permute-start.2) | collective-permute-done | bytes 131104 | tf_op jit(solution)/shard_map/ppermute | solution.py:382
  75.0 0.7 pair.1
  75.6 3.4 %all-to-all-start.3 = ((f32[8,40,128]{2,1,0:T(8,128)}), f32[8,40,128]{2,1,0:T(8,128)S(1)}, u32[]{:S(2)}, u32[]{:S(2)}) async-start(f32[8,40,128]{2,1,0:T(8,128)} %pair.1), calls=%async_computation.3 | async-start | bytes 327680 | tf_op jit(solution)/shard_map/all_to_all | solution.py:392
  79.1 2.3 %collective-permute-start.4 = (f32[136,128]{1,0:T(8,128)S(1)}, f32[136,128]{1,0:T(8,128)S(1)}, u32[]{:S(2)}, u32[]{:S(2)}) collective-permute-start(f32[136,128]{1,0:T(8,128)S(1)} %merge.4.mine_ref), channel_id=1, source_target_pairs={{0,64},{32,96},{64,0},{96,32},{128,192},{160,224},{192,128},{224,1... | collective-permute-start | bytes 208904 | tf_op jit(solution)/shard_map/ppermute | solution.py:337
  81.4 6.8 %collective-permute-done.4.got_ref = f32[136,128]{1,0:T(8,128)S(1)} collective-permute-done((f32[136,128]{1,0:T(8,128)S(1)}, f32[136,128]{1,0:T(8,128)S(1)}, u32[]{:S(2)}, u32[]{:S(2)}) %collective-permute-start.4) | collective-permute-done | bytes 69664 | tf_op jit(solution)/shard_map/ppermute | solution.py:337
  88.2 4.4 %collective-permute-start.5 = (f32[136,128]{1,0:T(8,128)S(1)}, f32[136,128]{1,0:T(8,128)S(1)}, u32[]{:S(2)}, u32[]{:S(2)}) collective-permute-start(f32[136,128]{1,0:T(8,128)S(1)} %merge.5.mine_ref), channel_id=1, source_target_pairs={{0,128},{32,160},{64,192},{96,224},{128,0},{160,32},{192,64},{224,... | collective-permute-start | bytes 208904 | tf_op jit(solution)/shard_map/ppermute | solution.py:337
  92.6 2.9 %collective-permute-done.5.got_ref = f32[136,128]{1,0:T(8,128)S(1)} collective-permute-done((f32[136,128]{1,0:T(8,128)S(1)}, f32[136,128]{1,0:T(8,128)S(1)}, u32[]{:S(2)}, u32[]{:S(2)}) %collective-permute-start.5) | collective-permute-done | bytes 69664 | tf_op jit(solution)/shard_map/ppermute | solution.py:337
  95.6 5.0 %solve.1.solved_ref = f32[136,128]{1,0:T(8,128)S(1)} custom-call(f32[136,128]{1,0:T(8,128)S(1)} %merge.5.mine_ref, f32[136,128]{1,0:T(8,128)S(1)} %collective-permute-done.5.got_ref, f32[12,128]{1,0:T(8,128)S(1)} %copy-done.1), custom_call_target="tpu_custom_call" | custom-call | flops 1000000000 | bytes 1000000 | tf_op jit(solution)/shard_map/solve/pallas_call | solution.py:393
  100.6 0.8 last.1
  (11 shorter events, 0.4 us)
Async XLA Ops:
  0.6 55.0 %copy-start.1 = (f32[12,128]{1,0:T(8,128)S(1)}, f32[12,128]{1,0:T(8,128)}, u32[]{:S(2)}) copy-start(f32[12,128]{1,0:T(8,128)} %c_ref.9) | copy-start | bytes 18436
  17.9 3.3 %collective-permute-start = (f32[8,32,128]{2,1,0:T(8,128)S(1)}, f32[8,32,128]{2,1,0:T(8,128)S(1)}, u32[]{:S(2)}, u32[]{:S(2)}) collective-permute-start(f32[8,32,128]{2,1,0:T(8,128)S(1)} %all_to_all.20.mine_ref), channel_id=1, source_target_pairs={{0,16},{16,0},{1,17},{17,1},{2,18},{18,2},{3,19},{19,3},{4,20},{20... | collective-permute-start | bytes 393224 | tf_op jit(solution)/shard_map/ppermute | solution.py:270
  21.2 0.7 copy-start
  43.9 11.7 %all-to-all-start.2 = ((f32[16,40,128]{2,1,0:T(8,128)}), f32[16,40,128]{2,1,0:T(8,128)S(1)}, u32[]{:S(2)}, u32[]{:S(2)}) async-start(f32[16,40,128]{2,1,0:T(8,128)} %sum.1), calls=%async_computation.2 | async-start | bytes 655360 | tf_op jit(solution)/shard_map/all_to_all | solution.py:297
  65.1 5.6 %collective-permute-start.1 = (f32[136,128]{1,0:T(8,128)S(1)}, f32[136,128]{1,0:T(8,128)S(1)}, u32[]{:S(2)}, u32[]{:S(2)}) collective-permute-start(f32[136,128]{1,0:T(8,128)S(1)} %get-tuple-element.9.mine_ref.message_ref), channel_id=1, source_target_pairs={{0,16},{16,0},{1,17},{17,1},{2,18},{18,2},{3,19},{19,3},{4,20},{20... | collective-permute-start | bytes 208904 | tf_op jit(solution)/shard_map/ppermute | solution.py:339
  73.5 1.4 %collective-permute-start.2 = (f32[256,128]{1,0:T(8,128)S(1)}, f32[256,128]{1,0:T(8,128)S(1)}, u32[]{:S(2)}, u32[]{:S(2)}) collective-permute-start(f32[256,128]{1,0:T(8,128)S(1)} %get-tuple-element.11), channel_id=1, source_target_pairs={{0,16},{16,0},{1,17},{17,1},{2,18},{18,2},{3,19},{19,3},{4,20},{20... | collective-permute-start | bytes 393224 | tf_op jit(solution)/shard_map/ppermute | solution.py:382
  73.6 5.4 %collective-permute-start.3 = (f32[136,128]{1,0:T(8,128)S(1)}, f32[136,128]{1,0:T(8,128)S(1)}, u32[]{:S(2)}, u32[]{:S(2)}) collective-permute-start(f32[136,128]{1,0:T(8,128)S(1)} %merge.3.pair_ref.mine_ref), channel_id=1, source_target_pairs={{0,32},{32,0},{64,96},{96,64},{128,160},{160,128},{192,224},{224,1... | collective-permute-start | bytes 208904 | tf_op jit(solution)/shard_map/ppermute | solution.py:337
  75.6 25.0 %all-to-all-start.3 = ((f32[8,40,128]{2,1,0:T(8,128)}), f32[8,40,128]{2,1,0:T(8,128)S(1)}, u32[]{:S(2)}, u32[]{:S(2)}) async-start(f32[8,40,128]{2,1,0:T(8,128)} %pair.1), calls=%async_computation.3 | async-start | bytes 327680 | tf_op jit(solution)/shard_map/all_to_all | solution.py:392
  79.1 9.1 %collective-permute-start.4 = (f32[136,128]{1,0:T(8,128)S(1)}, f32[136,128]{1,0:T(8,128)S(1)}, u32[]{:S(2)}, u32[]{:S(2)}) collective-permute-start(f32[136,128]{1,0:T(8,128)S(1)} %merge.4.mine_ref), channel_id=1, source_target_pairs={{0,64},{32,96},{64,0},{96,32},{128,192},{160,224},{192,128},{224,1... | collective-permute-start | bytes 208904 | tf_op jit(solution)/shard_map/ppermute | solution.py:337
  88.2 7.4 %collective-permute-start.5 = (f32[136,128]{1,0:T(8,128)S(1)}, f32[136,128]{1,0:T(8,128)S(1)}, u32[]{:S(2)}, u32[]{:S(2)}) collective-permute-start(f32[136,128]{1,0:T(8,128)S(1)} %merge.5.mine_ref), channel_id=1, source_target_pairs={{0,128},{32,160},{64,192},{96,224},{128,0},{160,32},{192,64},{224,... | collective-permute-start | bytes 208904 | tf_op jit(solution)/shard_map/ppermute | solution.py:337

commit v4 on v3

--- a/solution.py
+++ b/solution.py
@@ -17,7 +17,7 @@
 ROW = ("z", "core")
 COL = ("x", "y")
 TINY = 1e-30
-PARTS = 3
+HEAD = 3
 LARGE_MIB = 52
 WORK_MIB = 12
 
@@ -39,6 +39,12 @@
     return lax.dot_general(
         left, right, (((1,), (0,)), ((), ())), precision=HIGHEST,
         preferred_element_type=jnp.float32,
+    )
+
+
+def dot_turned(left, right):
+    return lax.dot_general(
+        left, right, (((1,), (1,)), ((), ())), preferred_element_type=jnp.float32
     )
 
 
@@ -102,35 +108,38 @@
     return jnp.concatenate(strips, axis=0)
 
 
-def first_kernel(core_ref, t_hbm, mine_ref, other_ref, c_hbm, out_ref, t_buf, b_block, b_both, total, c_ref, sems):
+def stage_kernel(in_ref, out_ref):
+    out_ref[...] = in_ref[...]
+
+
+def first_kernel(own_ref, t_hbm, mine_ref, other_ref, c_ref, out_ref, t_buf, b_block, total, sems):
     slices = t_hbm.shape[0]
-    pltpu.make_async_copy(c_hbm, c_ref, sems.at[slices]).start()
     for k in range(slices):
         pltpu.make_async_copy(t_hbm.at[k], t_buf.at[k], sems.at[k]).start()
-    core = core_ref[0]
+    core = own_ref[0]
     b_block[:, core] = mine_ref[...]
     b_block[:, 1 - core] = other_ref[...]
     width = c_ref.shape[1]
-    factor = b_block[...].reshape(b_both.shape[0], width)
-    b_high, b_low = split(factor)
-    b_both[:, :width] = b_high
-    b_both[:, width:] = b_low
+    factor = b_block[...].reshape(t_hbm.shape[2], width)
     gram = contract_rows(factor, factor)
     parts, rows, _ = out_ref.shape
     share = width // parts
     out_ref[:, rows - share :, :] = gram.reshape(parts, share, width)
-    pltpu.make_async_copy(c_hbm, c_ref, sems.at[slices]).wait()
+    turned = factor.T
+    c_turned = c_ref[...].T
     for k in range(slices):
+        w_high, w_low = split(turned * c_turned[:, k : k + 1])
+        w_both = jnp.concatenate([w_high, w_low], axis=0)
         pltpu.make_async_copy(t_hbm.at[k], t_buf.at[k], sems.at[k]).wait()
         t_high, t_low = split(t_buf[k])
-        main = jnp.dot(t_high, b_both[...], preferred_element_type=jnp.float32)
-        rest = jnp.dot(t_low, b_both[:, :width], preferred_element_type=jnp.float32)
-        term = (main[:, :width] + (main[:, width:] + rest)) * c_ref[k : k + 1, :]
+        main = dot_turned(w_both, t_high)
+        rest = dot_turned(w_high, t_low)
+        term = main[:width] + (main[width:] + rest)
         if k == 0:
             total[...] = term
         else:
             total[...] += term
-    out_ref[:, : rows - share, :] = total[...].reshape(parts, rows - share, width)
+    out_ref[:, : rows - share, :] = total[...].T.reshape(parts, rows - share, width)
 
 
 def sum_kernel(in_ref, out_ref):
@@ -141,7 +150,7 @@
     out_ref[...] = jnp.broadcast_to(total[None], out_ref.shape)
 
 
-def middle_kernel(where_ref, g_ref, c_ref, a_ref, scaled_ref, message_ref, block):
+def middle_kernel(own_ref, g_ref, c_ref, a_ref, scaled_ref, message_ref, block):
     parts, rows, width = g_ref.shape
     share = width // parts
     owned = rows - share
@@ -150,7 +159,7 @@
     solved = inverse(system)
     update = dot32(g_ref[:, :owned, :].reshape(parts * owned, width), solved)
     block[...] = update
-    start = pl.multiple_of(where_ref[0] * owned, owned)
+    start = pl.multiple_of(own_ref[1] * owned, owned)
     a_ref[...] = block[pl.ds(start, owned), :]
     most = jnp.max(jnp.abs(update), axis=0, keepdims=True)
     most = jnp.where(most > 0.0, most, TINY)
@@ -200,18 +209,13 @@
     partial_sum(begin, t_hbm, scaled_ref, c_ref, out_ref, t_buf, sems, True)
 
 
-def body_kernel(begin, t_hbm, scaled_ref, c_ref, in_ref, out_ref, t_buf, sems):
-    out_ref[...] = in_ref[...]
-    partial_sum(begin, t_hbm, scaled_ref, c_ref, out_ref, t_buf, sems, False)
-
-
-def tail_kernel(begin, core_ref, t_hbm, scaled_ref, c_ref, in_ref, message_ref, pair_ref, send_ref, keep_ref, total, halves, t_buf, sems):
+def tail_kernel(begin, own_ref, t_hbm, scaled_ref, c_ref, in_ref, message_ref, pair_ref, send_ref, keep_ref, total, halves, t_buf, sems):
     total[...] = in_ref[...]
     partial_sum(begin, t_hbm, scaled_ref, c_ref, total, t_buf, sems, False)
     width = scaled_ref.shape[1]
     scale = message_ref[width : width + 1, :] / pair_ref[width : width + 1, :]
     halves[...] = (total[...].T * scale).reshape(halves.shape)
-    core = core_ref[0]
+    core = own_ref[0]
     send_ref[...] = halves[:, 1 - core].reshape(send_ref.shape)
     keep_ref[...] = halves[:, core]
 
@@ -265,26 +269,34 @@
     f32 = jnp.float32
     shape = jax.ShapeDtypeStruct
 
+    small = limited(WORK_MIB)
+    swap = [(0, 1), (1, 0)]
+    own = jnp.stack([lax.axis_index("core"), lax.axis_index(COL)]).astype(jnp.int32)
     spread_b = jnp.broadcast_to(factor_b[None], (z_size,) + factor_b.shape)
     mine = lax.all_to_all(spread_b, "z", 0, 0, tiled=True)
-    other = lax.ppermute(mine, "core", [(0, 1), (1, 0)])
-    core = lax.axis_index("core").astype(jnp.int32).reshape(1)
+    other = lax.ppermute(mine, "core", swap)
+    staged_c = pl.pallas_call(
+        stage_kernel,
+        out_shape=pltpu.VMEM(factor_c.shape, f32),
+        in_specs=[VMEM],
+        out_specs=VMEM,
+        compiler_params=small,
+        name="stage",
+    )(factor_c)
     packed = pl.pallas_call(
         first_kernel,
         out_shape=shape((col_size, owned_a + share_a, width), f32),
-        in_specs=[SMEM, HBM, VMEM, VMEM, HBM],
+        in_specs=[SMEM, HBM, VMEM, VMEM, VMEM],
         out_specs=VMEM,
         scratch_shapes=[
             pltpu.VMEM(tensor.shape, f32),
             pltpu.VMEM((z_size, 2, owned_b, width), f32),
-            pltpu.VMEM((cols_block, 2 * width), jnp.bfloat16),
-            pltpu.VMEM((rows_block, width), f32),
-            pltpu.VMEM(factor_c.shape, f32),
-            pltpu.SemaphoreType.DMA((slices + 1,)),
+            pltpu.VMEM((width, rows_block), f32),
+            pltpu.SemaphoreType.DMA((slices,)),
         ],
         compiler_params=limited(LARGE_MIB),
         name="first",
-    )(core, tensor, mine, other, factor_c)
+    )(own, tensor, mine, other, staged_c)
     received = lax.all_to_all(packed, COL, 0, 0, tiled=True)
     summed = pl.pallas_call(
         sum_kernel,
@@ -295,7 +307,6 @@
         name="sum",
     )(received)
     gathered = lax.all_to_all(summed, COL, 0, 0, tiled=True)
-    where = lax.axis_index(COL).astype(jnp.int32).reshape(1)
     a_update, scaled, message = pl.pallas_call(
         middle_kernel,
         out_shape=(
@@ -308,20 +319,21 @@
         scratch_shapes=[pltpu.VMEM((rows_block, width), f32)],
         compiler_params=limited(WORK_MIB),
         name="middle",
-    )(where, gathered, factor_c)
-    small = limited(WORK_MIB)
-    swap = [(0, 1), (1, 0)]
-    per_part = slices // PARTS
-    part_cost = pl.CostEstimate(
-        flops=6 * tensor.size * width // PARTS,
-        bytes_accessed=4 * tensor.size // PARTS,
-        transcendentals=0,
-    )
-    part_scratch = [
-        pltpu.VMEM((per_part, rows_block, cols_block), f32),
-        pltpu.SemaphoreType.DMA((per_part,)),
-    ]
+    )(own, gathered, staged_c)
     running = shape((width, cols_block), f32)
+
+    def cost(count):
+        return pl.CostEstimate(
+            flops=6 * rows_block * cols_block * width * count,
+            bytes_accessed=4 * rows_block * cols_block * count,
+            transcendentals=0,
+        )
+
+    def part_scratch(count):
+        return [
+            pltpu.VMEM((count, rows_block, cols_block), f32),
+            pltpu.SemaphoreType.DMA((count,)),
+        ]
 
     def merged(mine, got):
         return pl.pallas_call(
@@ -342,27 +354,15 @@
         out_shape=running,
         in_specs=[HBM, VMEM, VMEM],
         out_specs=VMEM,
-        scratch_shapes=part_scratch,
+        scratch_shapes=part_scratch(HEAD),
         compiler_params=limited(LARGE_MIB),
-        cost_estimate=part_cost,
+        cost_estimate=cost(HEAD),
         name="head",
-    )(tensor, scaled, factor_c)
+    )(tensor, scaled, staged_c)
     pair = merged(message, got)
-    got = flipped(pair, 1)
-    total = pl.pallas_call(
-        functools.partial(body_kernel, per_part),
-        out_shape=running,
-        in_specs=[HBM, VMEM, VMEM, VMEM],
-        out_specs=VMEM,
-        scratch_shapes=part_scratch,
-        compiler_params=limited(LARGE_MIB),
-        cost_estimate=part_cost,
-        name="body",
-    )(tensor, scaled, factor_c, total)
-    quad = merged(pair, got)
-    got = flipped(quad, 2)
+    got = flipped(pair, 4)
     send, keep = pl.pallas_call(
-        functools.partial(tail_kernel, 2 * per_part),
+        functools.partial(tail_kernel, HEAD),
         out_shape=(
             shape((z_size * owned_b, width), f32),
             shape((z_size, owned_b, width), f32),
@@ -373,14 +373,16 @@
             pltpu.VMEM((width, cols_block), f32),
             pltpu.VMEM((z_size, 2, owned_b, width), f32),
         ]
-        + part_scratch,
+        + part_scratch(slices - HEAD),
         compiler_params=limited(LARGE_MIB),
-        cost_estimate=part_cost,
+        cost_estimate=cost(slices - HEAD),
         name="tail",
-    )(core, tensor, scaled, factor_c, total, message, pair)
+    )(own, tensor, scaled, staged_c, total, message, pair)
+    quad = merged(pair, got)
+    other_half = lax.ppermute(send, "core", swap)
+    got = flipped(quad, 2)
     octet = merged(quad, got)
-    other_half = lax.ppermute(send, "core", swap)
-    got = flipped(octet, 4)
+    got = flipped(octet, 1)
     outgoing = pl.pallas_call(
         pair_kernel,
         out_shape=shape((z_size, owned_b + 8, width), f32),
@@ -398,7 +400,7 @@
         compiler_params=small,
         cost_estimate=pl.CostEstimate(flops=10**9, bytes_accessed=10**6, transcendentals=0),
         name="solve",
-    )(octet, got, factor_c)
+    )(octet, got, staged_c)
     b_update = pl.pallas_call(
         last_kernel,
         out_shape=shape((owned_b, width), f32),

time: 102 us -> 97.5 us (0.956); the launches traced: 101 us -> 95.8 us
  blocking collectives: 31.1 us -> 42.6 us
  waiting for transfers between devices: 19.5 us -> 9.49 us
  starting transfers between devices: 19.8 us -> 14 us
  Pallas kernels: 28.8 us -> 27.5 us
    all_to_all x0 -> x1, blocking collectives: none -> 11.5 us  [per_device(): gathered = lax.all_to_all(summed, COL, 0, 0, tiled=True)]
    all_to_all x1 -> x0, waiting for transfers between devices: 7.66 us -> none  [per_device(): gathered = lax.all_to_all(summed, COL, 0, 0, tiled=True)]
    all_to_all x1 -> x0, starting transfers between devices: 4.06 us -> none  [per_device(): gathered = lax.all_to_all(summed, COL, 0, 0, tiled=True)]
    ppermute x3, starting transfers between devices: 6.95 us -> 3.05 us  [flipped(): return lax.ppermute(array, 'z', [(i, i ^ distance) for i in range(z_size)])]
    all_to_all x1, starting transfers between devices: 3.38 us -> 5.41 us  [per_device(): final = lax.all_to_all(outgoing, 'z', 0, 0, tiled=True)]
    ppermute x3, waiting for transfers between devices: 9.71 us -> 8.28 us  [flipped(): return lax.ppermute(array, 'z', [(i, i ^ distance) for i in range(z_size)])]
  transfers between devices with their start and end apart: 8 -> 7, of which waited for: 5 -> 4; matrix products, arithmetic and copies ran while one was open for 0% -> 0% of each run, Pallas kernels for 8% -> 8%
where the time goes in v4:
time: 97.5 us; the launch traced here: 95.8 us
  blocking collectives  42.6 us (44%)
  Pallas kernels  27.5 us (28%)
  starting transfers between devices  14 us (14%)
  waiting for transfers between devices  9.49 us (10%)
  local copies, waits for them, and re-layouts  1.42 us (1%)
    all_to_all x1, blocking collectives, per_device(): mine = lax.all_to_all(spread_b, 'z', 0, 0, tiled=True)  16.6 us
    all_to_all x1, blocking collectives, per_device(): received = lax.all_to_all(packed, COL, 0, 0, tiled=True)  14.5 us
    all_to_all x1, blocking collectives, per_device(): gathered = lax.all_to_all(summed, COL, 0, 0, tiled=True)  11.5 us
    ppermute x3, waiting for transfers between devices, flipped(): return lax.ppermute(array, 'z', [(i, i ^ distance) for i in range(z_size)])  8.28 us
    pallas_call x1, Pallas kernels, per_device(): pl.pallas_call(middle_kernel, out_shape=(shape((owned_a, width), f32), sh...  7.42 us
    pallas_call x1, Pallas kernels, per_device(): pl.pallas_call(first_kernel, out_shape=shape((col_size, owned_a + share_a...  6.4 us
    all_to_all x1, starting transfers between devices, per_device(): final = lax.all_to_all(outgoing, 'z', 0, 0, tiled=True)  5.41 us
    pallas_call x1, Pallas kernels, per_device(): pl.pallas_call(solve_kernel, out_shape=shape(message.shape, f32), in_spec...  5.04 us
  transfers between devices with their start and end apart: 7, of which 4 were waited for; matrix products, arithmetic and copies ran while one was open for 0% of the time, Pallas kernels for 8%

profile of v4, /device:TPU:1, one launch (start us, length us, event | category | flops | bytes accessed | tf_op | source)
XLA Modules:
  0.0 95.8 jit_solution(783640397262756921)
XLA Ops:
  0.6 0.7 broadcast_in_dim.2
  1.4 16.6 %all_to_all.20.mine_ref = f32[8,32,128]{2,1,0:T(8,128)S(1)} all-to-all(f32[8,32,128]{2,1,0:T(8,128)S(1)} %broadcast_in_dim.2), channel_id=1, replica_groups=mesh['z'=8,'core'=2,'x'=4,'y'=4] {'z'}, dimensions={0} | all-to-all | bytes 262144 | tf_op jit(solution)/shard_map/all_to_all | solution.py:276
  17.9 2.3 %collective-permute-start = (f32[8,32,128]{2,1,0:T(8,128)S(1)}, f32[8,32,128]{2,1,0:T(8,128)S(1)}, u32[]{:S(2)}, u32[]{:S(2)}) collective-permute-start(f32[8,32,128]{2,1,0:T(8,128)S(1)} %all_to_all.20.mine_ref), channel_id=1, source_target_pairs={{0,16},{16,0},{1,17},{17,1},{2,18},{18,2},{3,19},{19,3},{4,20},{20... | collective-permute-start | bytes 393224 | tf_op jit(solution)/shard_map/ppermute | solution.py:277
  20.2 0.7 copy-done
  20.9 0.1 pad_add_fusion.own_ref
  21.0 0.2 collective-permute-done.other_ref
  21.2 6.4 %first.1 = f32[16,40,128]{2,1,0:T(8,128)S(1)} custom-call(s32[2]{0:T(128)S(1)} %pad_add_fusion.own_ref, f32[12,512,512]{2,1,0:T(8,128)} %t_hbm.5, f32[8,32,128]{2,1,0:T(8,128)S(1)} %all_to_all.20.mine_ref, f32[8,32,128]{2,1,0:T(8,128)S(1)} %collective-permute-done.other_ref, f32[12,128]{1,0:T(8,128)S(1)} %stage.1.c_ref), custom_call_target="tpu_custom_call" | custom-call | tf_op jit(solution)/shard_map/first/pallas_call | solution.py:286
  27.6 14.5 %all_to_all.21.in_ref = f32[16,40,128]{2,1,0:T(8,128)S(1)} all-to-all(f32[16,40,128]{2,1,0:T(8,128)S(1)} %first.1), channel_id=1, replica_groups=mesh['z'=8,'core'=2,'x'=4,'y'=4] {'x','y'}, dimensions={0} | all-to-all | bytes 655360 | tf_op jit(solution)/shard_map/all_to_all | solution.py:300
  42.2 11.5 %all_to_all.22.g_ref = f32[16,40,128]{2,1,0:T(8,128)S(1)} all-to-all(f32[16,40,128]{2,1,0:T(8,128)S(1)} %sum.1), channel_id=1, replica_groups=mesh['z'=8,'core'=2,'x'=4,'y'=4] {'x','y'}, dimensions={0} | all-to-all | bytes 655360 | tf_op jit(solution)/shard_map/all_to_all | solution.py:309
  53.7 7.4 %middle.1 = (f32[32,128]{1,0:T(8,128)}, f32[512,128]{1,0:T(8,128)S(1)}, f32[136,128]{1,0:T(8,128)S(1)}) custom-call(s32[2]{0:T(128)S(1)} %pad_add_fusion.own_ref, f32[16,40,128]{2,1,0:T(8,128)S(1)} %all_to_all.22.g_ref, f32[12,128]{1,0:T(8,128)S(1)} %stage.1.c_ref), custom_call_target="tpu_custom_call" | custom-call | tf_op jit(solution)/shard_map/middle/pallas_call | solution.py:310
  61.1 3.1 %collective-permute-start.1 = (f32[136,128]{1,0:T(8,128)S(1)}, f32[136,128]{1,0:T(8,128)S(1)}, u32[]{:S(2)}, u32[]{:S(2)}) collective-permute-start(f32[136,128]{1,0:T(8,128)S(1)} %get-tuple-element.9.mine_ref.message_ref), channel_id=1, source_target_pairs={{0,16},{16,0},{1,17},{17,1},{2,18},{18,2},{3,19},{19,3},{4,20},{20... | collective-permute-start | bytes 208904 | tf_op jit(solution)/shard_map/ppermute | solution.py:351
  64.2 2.3 %head.1.in_ref = f32[128,512]{1,0:T(8,128)S(1)} custom-call(f32[12,512,512]{2,1,0:T(8,128)} %t_hbm.5, f32[512,128]{1,0:T(8,128)S(1)} %get-tuple-element.8.scaled_ref, f32[12,128]{1,0:T(8,128)S(1)} %stage.1.c_ref), custom_call_target="tpu_custom_call" | custom-call | flops 603979776 | bytes 3145728 | tf_op jit(solution)/shard_map/head/pallas_call | solution.py:352
  66.5 4.8 %tail.1 = (f32[256,128]{1,0:T(8,128)S(1)}, f32[8,32,128]{2,1,0:T(8,128)S(1)}) custom-call(s32[2]{0:T(128)S(1)} %pad_add_fusion.own_ref, f32[12,512,512]{2,1,0:T(8,128)} %t_hbm.5, f32[512,128]{1,0:T(8,128)S(1)} %get-tuple-element.8.scaled_ref, f32[12,128]{1,0:T(8,128)S(1)} %stage.1.c_ref, f32[128,512]{1,0:T(8,128)S(1)} %head.1.in_ref, ...), custom_call_target="tpu_custom_call" | custom-call | flops 1811939328 | bytes 9437184 | tf_op jit(solution)/shard_map/tail/pallas_call | solution.py:364
  71.4 0.1 collective-permute-start.2
  71.5 0.3 collective-permute-start.3
  71.8 1.0 %collective-permute-done.2.got_ref = f32[256,128]{1,0:T(8,128)S(1)} collective-permute-done((f32[256,128]{1,0:T(8,128)S(1)}, f32[256,128]{1,0:T(8,128)S(1)}, u32[]{:S(2)}, u32[]{:S(2)}) %collective-permute-start.2) | collective-permute-done | bytes 131104 | tf_op jit(solution)/shard_map/ppermute | solution.py:382
  72.8 0.7 pair.1
  73.5 5.4 %all-to-all-start.3 = ((f32[8,40,128]{2,1,0:T(8,128)}), f32[8,40,128]{2,1,0:T(8,128)S(1)}, u32[]{:S(2)}, u32[]{:S(2)}) async-start(f32[8,40,128]{2,1,0:T(8,128)} %pair.1), calls=%async_computation.3 | async-start | bytes 327680 | tf_op jit(solution)/shard_map/all_to_all | solution.py:394
  78.9 2.4 %collective-permute-start.4 = (f32[136,128]{1,0:T(8,128)S(1)}, f32[136,128]{1,0:T(8,128)S(1)}, u32[]{:S(2)}, u32[]{:S(2)}) collective-permute-start(f32[136,128]{1,0:T(8,128)S(1)} %merge.4.mine_ref), channel_id=1, source_target_pairs={{0,64},{32,96},{64,0},{96,32},{128,192},{160,224},{192,128},{224,1... | collective-permute-start | bytes 208904 | tf_op jit(solution)/shard_map/ppermute | solution.py:349
  81.4 5.0 %collective-permute-done.4.got_ref = f32[136,128]{1,0:T(8,128)S(1)} collective-permute-done((f32[136,128]{1,0:T(8,128)S(1)}, f32[136,128]{1,0:T(8,128)S(1)}, u32[]{:S(2)}, u32[]{:S(2)}) %collective-permute-start.4) | collective-permute-done | bytes 69664 | tf_op jit(solution)/shard_map/ppermute | solution.py:349
  86.4 0.3 collective-permute-start.5
  86.7 3.3 %collective-permute-done.5.got_ref = f32[136,128]{1,0:T(8,128)S(1)} collective-permute-done((f32[136,128]{1,0:T(8,128)S(1)}, f32[136,128]{1,0:T(8,128)S(1)}, u32[]{:S(2)}, u32[]{:S(2)}) %collective-permute-start.5) | collective-permute-done | bytes 69664 | tf_op jit(solution)/shard_map/ppermute | solution.py:349
  89.9 5.0 %solve.1.solved_ref = f32[136,128]{1,0:T(8,128)S(1)} custom-call(f32[136,128]{1,0:T(8,128)S(1)} %merge.5.mine_ref, f32[136,128]{1,0:T(8,128)S(1)} %collective-permute-done.5.got_ref, f32[12,128]{1,0:T(8,128)S(1)} %stage.1.c_ref), custom_call_target="tpu_custom_call" | custom-call | flops 1000000000 | bytes 1000000 | tf_op jit(solution)/shard_map/solve/pallas_call | solution.py:395
  95.0 0.8 last.1
  (9 shorter events, 0.1 us)
Async XLA Ops:
  17.9 3.3 %collective-permute-start = (f32[8,32,128]{2,1,0:T(8,128)S(1)}, f32[8,32,128]{2,1,0:T(8,128)S(1)}, u32[]{:S(2)}, u32[]{:S(2)}) collective-permute-start(f32[8,32,128]{2,1,0:T(8,128)S(1)} %all_to_all.20.mine_ref), channel_id=1, source_target_pairs={{0,16},{16,0},{1,17},{17,1},{2,18},{18,2},{3,19},{19,3},{4,20},{20... | collective-permute-start | bytes 393224 | tf_op jit(solution)/shard_map/ppermute | solution.py:277
  20.2 0.7 copy-start
  61.1 5.4 %collective-permute-start.1 = (f32[136,128]{1,0:T(8,128)S(1)}, f32[136,128]{1,0:T(8,128)S(1)}, u32[]{:S(2)}, u32[]{:S(2)}) collective-permute-start(f32[136,128]{1,0:T(8,128)S(1)} %get-tuple-element.9.mine_ref.message_ref), channel_id=1, source_target_pairs={{0,16},{16,0},{1,17},{17,1},{2,18},{18,2},{3,19},{19,3},{4,20},{20... | collective-permute-start | bytes 208904 | tf_op jit(solution)/shard_map/ppermute | solution.py:351
  71.4 1.4 %collective-permute-start.2 = (f32[256,128]{1,0:T(8,128)S(1)}, f32[256,128]{1,0:T(8,128)S(1)}, u32[]{:S(2)}, u32[]{:S(2)}) collective-permute-start(f32[256,128]{1,0:T(8,128)S(1)} %get-tuple-element.11), channel_id=1, source_target_pairs={{0,16},{16,0},{1,17},{17,1},{2,18},{18,2},{3,19},{19,3},{4,20},{20... | collective-permute-start | bytes 393224 | tf_op jit(solution)/shard_map/ppermute | solution.py:382
  71.5 7.4 %collective-permute-start.3 = (f32[136,128]{1,0:T(8,128)S(1)}, f32[136,128]{1,0:T(8,128)S(1)}, u32[]{:S(2)}, u32[]{:S(2)}) collective-permute-start(f32[136,128]{1,0:T(8,128)S(1)} %merge.3.pair_ref.mine_ref), channel_id=1, source_target_pairs={{0,128},{32,160},{64,192},{96,224},{128,0},{160,32},{192,64},{224,... | collective-permute-start | bytes 208904 | tf_op jit(solution)/shard_map/ppermute | solution.py:349
  73.5 21.5 %all-to-all-start.3 = ((f32[8,40,128]{2,1,0:T(8,128)}), f32[8,40,128]{2,1,0:T(8,128)S(1)}, u32[]{:S(2)}, u32[]{:S(2)}) async-start(f32[8,40,128]{2,1,0:T(8,128)} %pair.1), calls=%async_computation.3 | async-start | bytes 327680 | tf_op jit(solution)/shard_map/all_to_all | solution.py:394
  78.9 7.4 %collective-permute-start.4 = (f32[136,128]{1,0:T(8,128)S(1)}, f32[136,128]{1,0:T(8,128)S(1)}, u32[]{:S(2)}, u32[]{:S(2)}) collective-permute-start(f32[136,128]{1,0:T(8,128)S(1)} %merge.4.mine_ref), channel_id=1, source_target_pairs={{0,64},{32,96},{64,0},{96,32},{128,192},{160,224},{192,128},{224,1... | collective-permute-start | bytes 208904 | tf_op jit(solution)/shard_map/ppermute | solution.py:349
  86.4 3.6 %collective-permute-start.5 = (f32[136,128]{1,0:T(8,128)S(1)}, f32[136,128]{1,0:T(8,128)S(1)}, u32[]{:S(2)}, u32[]{:S(2)}) collective-permute-start(f32[136,128]{1,0:T(8,128)S(1)} %merge.5.mine_ref), channel_id=1, source_target_pairs={{0,32},{32,0},{64,96},{96,64},{128,160},{160,128},{192,224},{224,1... | collective-permute-start | bytes 208904 | tf_op jit(solution)/shard_map/ppermute | solution.py:349

commit v5 on v4

--- a/solution.py
+++ b/solution.py
@@ -1,5 +1,3 @@
-import functools
-
 import jax
 import jax.numpy as jnp
 from jax import lax
@@ -17,7 +15,6 @@
 ROW = ("z", "core")
 COL = ("x", "y")
 TINY = 1e-30
-HEAD = 3
 LARGE_MIB = 52
 WORK_MIB = 12
 
@@ -163,7 +160,7 @@
     a_ref[...] = block[pl.ds(start, owned), :]
     most = jnp.max(jnp.abs(update), axis=0, keepdims=True)
     most = jnp.where(most > 0.0, most, TINY)
-    scaled = update / most
+    scaled = update * (1.0 / most)
     scaled_ref[...] = scaled
     message_ref[:width, :] = contract_rows(update, scaled)
     message_ref[width:, :] = jnp.broadcast_to(most, (message_ref.shape[0] - width, width))
@@ -184,35 +181,25 @@
     out_ref[width:, :] = jnp.broadcast_to(most, (out_ref.shape[0] - width, width))
 
 
-def partial_sum(begin, t_hbm, scaled_ref, c_ref, total, t_buf, sems, fresh):
-    slices = t_buf.shape[0]
+def second_kernel(own_ref, t_hbm, scaled_ref, c_ref, message_ref, pair_ref, send_ref, keep_ref, total, halves, t_buf, sems):
+    slices = t_hbm.shape[0]
     for k in range(slices):
-        pltpu.make_async_copy(t_hbm.at[begin + k], t_buf.at[k], sems.at[k]).start()
+        pltpu.make_async_copy(t_hbm.at[k], t_buf.at[k], sems.at[k]).start()
     turned = scaled_ref[...].T
     width = turned.shape[0]
     c_turned = c_ref[...].T
     for k in range(slices):
-        w_high, w_low = split(turned * c_turned[:, begin + k : begin + k + 1])
+        w_high, w_low = split(turned * c_turned[:, k : k + 1])
         w_both = jnp.concatenate([w_high, w_low], axis=0)
-        pltpu.make_async_copy(t_hbm.at[begin + k], t_buf.at[k], sems.at[k]).wait()
+        pltpu.make_async_copy(t_hbm.at[k], t_buf.at[k], sems.at[k]).wait()
         t_high, t_low = split(t_buf[k])
         main = jnp.dot(w_both, t_high, preferred_element_type=jnp.float32)
         rest = jnp.dot(w_high, t_low, preferred_element_type=jnp.float32)
         term = main[:width] + (main[width:] + rest)
-        if fresh and k == 0:
+        if k == 0:
             total[...] = term
         else:
             total[...] += term
-
-
-def head_kernel(begin, t_hbm, scaled_ref, c_ref, out_ref, t_buf, sems):
-    partial_sum(begin, t_hbm, scaled_ref, c_ref, out_ref, t_buf, sems, True)
-
-
-def tail_kernel(begin, own_ref, t_hbm, scaled_ref, c_ref, in_ref, message_ref, pair_ref, send_ref, keep_ref, total, halves, t_buf, sems):
-    total[...] = in_ref[...]
-    partial_sum(begin, t_hbm, scaled_ref, c_ref, total, t_buf, sems, False)
-    width = scaled_ref.shape[1]
     scale = message_ref[width : width + 1, :] / pair_ref[width : width + 1, :]
     halves[...] = (total[...].T * scale).reshape(halves.shape)
     core = own_ref[0]
@@ -320,20 +307,6 @@
         compiler_params=limited(WORK_MIB),
         name="middle",
     )(own, gathered, staged_c)
-    running = shape((width, cols_block), f32)
-
-    def cost(count):
-        return pl.CostEstimate(
-            flops=6 * rows_block * cols_block * width * count,
-            bytes_accessed=4 * rows_block * cols_block * count,
-            transcendentals=0,
-        )
-
-    def part_scratch(count):
-        return [
-            pltpu.VMEM((count, rows_block, cols_block), f32),
-            pltpu.SemaphoreType.DMA((count,)),
-        ]
 
     def merged(mine, got):
         return pl.pallas_call(
@@ -349,40 +322,33 @@
         return lax.ppermute(array, "z", [(i, i ^ distance) for i in range(z_size)])
 
     got = lax.ppermute(message, "core", swap)
-    total = pl.pallas_call(
-        functools.partial(head_kernel, 0),
-        out_shape=running,
-        in_specs=[HBM, VMEM, VMEM],
-        out_specs=VMEM,
-        scratch_shapes=part_scratch(HEAD),
-        compiler_params=limited(LARGE_MIB),
-        cost_estimate=cost(HEAD),
-        name="head",
-    )(tensor, scaled, staged_c)
     pair = merged(message, got)
     got = flipped(pair, 4)
     send, keep = pl.pallas_call(
-        functools.partial(tail_kernel, HEAD),
+        second_kernel,
         out_shape=(
             shape((z_size * owned_b, width), f32),
             shape((z_size, owned_b, width), f32),
         ),
-        in_specs=[SMEM, HBM] + [VMEM] * 5,
+        in_specs=[SMEM, HBM] + [VMEM] * 4,
         out_specs=(VMEM, VMEM),
         scratch_shapes=[
             pltpu.VMEM((width, cols_block), f32),
             pltpu.VMEM((z_size, 2, owned_b, width), f32),
-        ]
-        + part_scratch(slices - HEAD),
+            pltpu.VMEM(tensor.shape, f32),
+            pltpu.SemaphoreType.DMA((slices,)),
+        ],
         compiler_params=limited(LARGE_MIB),
-        cost_estimate=cost(slices - HEAD),
-        name="tail",
-    )(own, tensor, scaled, staged_c, total, message, pair)
+        cost_estimate=pl.CostEstimate(
+            flops=6 * tensor.size * width, bytes_accessed=4 * tensor.size, transcendentals=0
+        ),
+        name="second",
+    )(own, tensor, scaled, staged_c, message, pair)
     quad = merged(pair, got)
     other_half = lax.ppermute(send, "core", swap)
-    got = flipped(quad, 2)
+    got = flipped(quad, 1)
     octet = merged(quad, got)
-    got = flipped(octet, 1)
+    got = flipped(octet, 2)
     outgoing = pl.pallas_call(
         pair_kernel,
         out_shape=shape((z_size, owned_b + 8, width), f32),

time: 97.5 us -> 95.8 us (0.983); the launches traced: 95.8 us -> 95.3 us
  Pallas kernels: 27.5 us -> 26.2 us
    pallas_call x2 -> x1, Pallas kernels: 7.1 us -> 5.75 us  [per_device(): pl.pallas_call(second_kernel, out_shape=(shape((z_size * owned_b, width),...]
  transfers between devices with their start and end apart: 7 -> 7, of which waited for: 4 -> 6; matrix products, arithmetic and copies ran while one was open for 0% -> 0% of each run, Pallas kernels for 8% -> 6%
where the time goes in v5:
time: 95.8 us; the launch traced here: 95.3 us
  blocking collectives  42.6 us (44%)
  Pallas kernels  26.2 us (27%)
  starting transfers between devices  14.2 us (15%)
  waiting for transfers between devices  10.2 us (11%)
  local copies, waits for them, and re-layouts  1.42 us (1%)
    all_to_all x1, blocking collectives, per_device(): mine = lax.all_to_all(spread_b, 'z', 0, 0, tiled=True)  16.6 us
    all_to_all x1, blocking collectives, per_device(): received = lax.all_to_all(packed, COL, 0, 0, tiled=True)  14.5 us
    all_to_all x1, blocking collectives, per_device(): gathered = lax.all_to_all(summed, COL, 0, 0, tiled=True)  11.5 us
    ppermute x3, waiting for transfers between devices, flipped(): return lax.ppermute(array, 'z', [(i, i ^ distance) for i in range(z_size)])  8.31 us
    pallas_call x1, Pallas kernels, per_device(): pl.pallas_call(middle_kernel, out_shape=(shape((owned_a, width), f32), sh...  7.42 us
    pallas_call x1, Pallas kernels, per_device(): pl.pallas_call(first_kernel, out_shape=shape((col_size, owned_a + share_a...  6.4 us
    pallas_call x1, Pallas kernels, per_device(): pl.pallas_call(second_kernel, out_shape=(shape((z_size * owned_b, width),...  5.75 us
    all_to_all x1, starting transfers between devices, per_device(): final = lax.all_to_all(outgoing, 'z', 0, 0, tiled=True)  5.66 us
  transfers between devices with their start and end apart: 7, of which 6 were waited for; matrix products, arithmetic and copies ran while one was open for 0% of the time, Pallas kernels for 6%

profile of v5, /device:TPU:1, one launch (start us, length us, event | category | flops | bytes accessed | tf_op | source)
XLA Modules:
  0.0 95.3 jit_solution(135006464362392541)
XLA Ops:
  0.6 0.7 broadcast_in_dim.2
  1.4 16.6 %all_to_all.20.mine_ref = f32[8,32,128]{2,1,0:T(8,128)S(1)} all-to-all(f32[8,32,128]{2,1,0:T(8,128)S(1)} %broadcast_in_dim.2), channel_id=1, replica_groups=mesh['z'=8,'core'=2,'x'=4,'y'=4] {'z'}, dimensions={0} | all-to-all | bytes 262144 | tf_op jit(solution)/shard_map/all_to_all | solution.py:263
  17.9 2.3 %collective-permute-start = (f32[8,32,128]{2,1,0:T(8,128)S(1)}, f32[8,32,128]{2,1,0:T(8,128)S(1)}, u32[]{:S(2)}, u32[]{:S(2)}) collective-permute-start(f32[8,32,128]{2,1,0:T(8,128)S(1)} %all_to_all.20.mine_ref), channel_id=1, source_target_pairs={{0,16},{16,0},{1,17},{17,1},{2,18},{18,2},{3,19},{19,3},{4,20},{20... | collective-permute-start | bytes 393224 | tf_op jit(solution)/shard_map/ppermute | solution.py:264
  20.2 0.7 copy-done
  21.0 0.2 collective-permute-done.other_ref
  21.2 6.4 %first.1 = f32[16,40,128]{2,1,0:T(8,128)S(1)} custom-call(s32[2]{0:T(128)S(1)} %pad_add_fusion.own_ref, f32[12,512,512]{2,1,0:T(8,128)} %t_hbm.3, f32[8,32,128]{2,1,0:T(8,128)S(1)} %all_to_all.20.mine_ref, f32[8,32,128]{2,1,0:T(8,128)S(1)} %collective-permute-done.other_ref, f32[12,128]{1,0:T(8,128)S(1)} %stage.1.c_ref), custom_call_target="tpu_custom_call" | custom-call | tf_op jit(solution)/shard_map/first/pallas_call | solution.py:273
  27.6 14.5 %all_to_all.21.in_ref = f32[16,40,128]{2,1,0:T(8,128)S(1)} all-to-all(f32[16,40,128]{2,1,0:T(8,128)S(1)} %first.1), channel_id=1, replica_groups=mesh['z'=8,'core'=2,'x'=4,'y'=4] {'x','y'}, dimensions={0} | all-to-all | bytes 655360 | tf_op jit(solution)/shard_map/all_to_all | solution.py:287
  42.2 11.5 %all_to_all.22.g_ref = f32[16,40,128]{2,1,0:T(8,128)S(1)} all-to-all(f32[16,40,128]{2,1,0:T(8,128)S(1)} %sum.1), channel_id=1, replica_groups=mesh['z'=8,'core'=2,'x'=4,'y'=4] {'x','y'}, dimensions={0} | all-to-all | bytes 655360 | tf_op jit(solution)/shard_map/all_to_all | solution.py:296
  53.7 7.4 %middle.1 = (f32[32,128]{1,0:T(8,128)}, f32[512,128]{1,0:T(8,128)S(1)}, f32[136,128]{1,0:T(8,128)S(1)}) custom-call(s32[2]{0:T(128)S(1)} %pad_add_fusion.own_ref, f32[16,40,128]{2,1,0:T(8,128)S(1)} %all_to_all.22.g_ref, f32[12,128]{1,0:T(8,128)S(1)} %stage.1.c_ref), custom_call_target="tpu_custom_call" | custom-call | tf_op jit(solution)/shard_map/middle/pallas_call | solution.py:297
  61.1 3.1 %collective-permute-start.1 = (f32[136,128]{1,0:T(8,128)S(1)}, f32[136,128]{1,0:T(8,128)S(1)}, u32[]{:S(2)}, u32[]{:S(2)}) collective-permute-start(f32[136,128]{1,0:T(8,128)S(1)} %get-tuple-element.9.mine_ref.message_ref), channel_id=1, source_target_pairs={{0,16},{16,0},{1,17},{17,1},{2,18},{18,2},{3,19},{19,3},{4,20},{20... | collective-permute-start | bytes 208904 | tf_op jit(solution)/shard_map/ppermute | solution.py:324
  64.2 0.9 collective-permute-done.1.got_ref
  65.2 5.8 %second.1 = (f32[256,128]{1,0:T(8,128)S(1)}, f32[8,32,128]{2,1,0:T(8,128)S(1)}) custom-call(s32[2]{0:T(128)S(1)} %pad_add_fusion.own_ref, f32[12,512,512]{2,1,0:T(8,128)} %t_hbm.3, f32[512,128]{1,0:T(8,128)S(1)} %get-tuple-element.8.scaled_ref, f32[12,128]{1,0:T(8,128)S(1)} %stage.1.c_ref, f32[136,128]{1,0:T(8,128)S(1)} %get-tuple-element.9.mine_ref.message_ref, ...), custom_call_target="tpu_custom_call" | custom-call | flops 2415919104 | bytes 12582912 | tf_op jit(solution)/shard_map/second/pallas_call | solution.py:327
  70.9 0.4 collective-permute-start.2
  71.3 0.3 collective-permute-start.3
  71.6 0.7 collective-permute-done.2.got_ref
  72.3 0.7 pair.1
  73.0 5.7 %all-to-all-start.3 = ((f32[8,40,128]{2,1,0:T(8,128)}), f32[8,40,128]{2,1,0:T(8,128)S(1)}, u32[]{:S(2)}, u32[]{:S(2)}) async-start(f32[8,40,128]{2,1,0:T(8,128)} %pair.1), calls=%async_computation.3 | async-start | bytes 327680 | tf_op jit(solution)/shard_map/all_to_all | solution.py:360
  78.7 0.3 collective-permute-done.3.got_ref
  79.0 1.2 %collective-permute-start.4 = (f32[136,128]{1,0:T(8,128)S(1)}, f32[136,128]{1,0:T(8,128)S(1)}, u32[]{:S(2)}, u32[]{:S(2)}) collective-permute-start(f32[136,128]{1,0:T(8,128)S(1)} %merge.4.mine_ref), channel_id=1, source_target_pairs={{0,32},{32,0},{64,96},{96,64},{128,160},{160,128},{192,224},{224,1... | collective-permute-start | bytes 208904 | tf_op jit(solution)/shard_map/ppermute | solution.py:322
  80.2 4.7 %collective-permute-done.4.got_ref = f32[136,128]{1,0:T(8,128)S(1)} collective-permute-done((f32[136,128]{1,0:T(8,128)S(1)}, f32[136,128]{1,0:T(8,128)S(1)}, u32[]{:S(2)}, u32[]{:S(2)}) %collective-permute-start.4) | collective-permute-done | bytes 69664 | tf_op jit(solution)/shard_map/ppermute | solution.py:322
  85.0 1.3 %collective-permute-start.5 = (f32[136,128]{1,0:T(8,128)S(1)}, f32[136,128]{1,0:T(8,128)S(1)}, u32[]{:S(2)}, u32[]{:S(2)}) collective-permute-start(f32[136,128]{1,0:T(8,128)S(1)} %merge.5.mine_ref), channel_id=1, source_target_pairs={{0,64},{32,96},{64,0},{96,32},{128,192},{160,224},{192,128},{224,1... | collective-permute-start | bytes 208904 | tf_op jit(solution)/shard_map/ppermute | solution.py:322
  86.3 3.2 %collective-permute-done.5.got_ref = f32[136,128]{1,0:T(8,128)S(1)} collective-permute-done((f32[136,128]{1,0:T(8,128)S(1)}, f32[136,128]{1,0:T(8,128)S(1)}, u32[]{:S(2)}, u32[]{:S(2)}) %collective-permute-start.5) | collective-permute-done | bytes 69664 | tf_op jit(solution)/shard_map/ppermute | solution.py:322
  89.5 5.0 %solve.1.solved_ref = f32[136,128]{1,0:T(8,128)S(1)} custom-call(f32[136,128]{1,0:T(8,128)S(1)} %merge.5.mine_ref, f32[136,128]{1,0:T(8,128)S(1)} %collective-permute-done.5.got_ref, f32[12,128]{1,0:T(8,128)S(1)} %stage.1.c_ref), custom_call_target="tpu_custom_call" | custom-call | flops 1000000000 | bytes 1000000 | tf_op jit(solution)/shard_map/solve/pallas_call | solution.py:361
  94.6 0.8 last.1
  (8 shorter events, 0.2 us)
Async XLA Ops:
  17.9 3.3 %collective-permute-start = (f32[8,32,128]{2,1,0:T(8,128)S(1)}, f32[8,32,128]{2,1,0:T(8,128)S(1)}, u32[]{:S(2)}, u32[]{:S(2)}) collective-permute-start(f32[8,32,128]{2,1,0:T(8,128)S(1)} %all_to_all.20.mine_ref), channel_id=1, source_target_pairs={{0,16},{16,0},{1,17},{17,1},{2,18},{18,2},{3,19},{19,3},{4,20},{20... | collective-permute-start | bytes 393224 | tf_op jit(solution)/shard_map/ppermute | solution.py:264
  20.2 0.7 copy-start
  61.1 4.0 %collective-permute-start.1 = (f32[136,128]{1,0:T(8,128)S(1)}, f32[136,128]{1,0:T(8,128)S(1)}, u32[]{:S(2)}, u32[]{:S(2)}) collective-permute-start(f32[136,128]{1,0:T(8,128)S(1)} %get-tuple-element.9.mine_ref.message_ref), channel_id=1, source_target_pairs={{0,16},{16,0},{1,17},{17,1},{2,18},{18,2},{3,19},{19,3},{4,20},{20... | collective-permute-start | bytes 208904 | tf_op jit(solution)/shard_map/ppermute | solution.py:324
  70.9 1.4 %collective-permute-start.2 = (f32[256,128]{1,0:T(8,128)S(1)}, f32[256,128]{1,0:T(8,128)S(1)}, u32[]{:S(2)}, u32[]{:S(2)}) collective-permute-start(f32[256,128]{1,0:T(8,128)S(1)} %get-tuple-element.11), channel_id=1, source_target_pairs={{0,16},{16,0},{1,17},{17,1},{2,18},{18,2},{3,19},{19,3},{4,20},{20... | collective-permute-start | bytes 393224 | tf_op jit(solution)/shard_map/ppermute | solution.py:348
  71.3 7.7 %collective-permute-start.3 = (f32[136,128]{1,0:T(8,128)S(1)}, f32[136,128]{1,0:T(8,128)S(1)}, u32[]{:S(2)}, u32[]{:S(2)}) collective-permute-start(f32[136,128]{1,0:T(8,128)S(1)} %merge.3.pair_ref.mine_ref), channel_id=1, source_target_pairs={{0,128},{32,160},{64,192},{96,224},{128,0},{160,32},{192,64},{224,... | collective-permute-start | bytes 208904 | tf_op jit(solution)/shard_map/ppermute | solution.py:322
  73.0 21.5 %all-to-all-start.3 = ((f32[8,40,128]{2,1,0:T(8,128)}), f32[8,40,128]{2,1,0:T(8,128)S(1)}, u32[]{:S(2)}, u32[]{:S(2)}) async-start(f32[8,40,128]{2,1,0:T(8,128)} %pair.1), calls=%async_computation.3 | async-start | bytes 327680 | tf_op jit(solution)/shard_map/all_to_all | solution.py:360
  79.0 6.0 %collective-permute-start.4 = (f32[136,128]{1,0:T(8,128)S(1)}, f32[136,128]{1,0:T(8,128)S(1)}, u32[]{:S(2)}, u32[]{:S(2)}) collective-permute-start(f32[136,128]{1,0:T(8,128)S(1)} %merge.4.mine_ref), channel_id=1, source_target_pairs={{0,32},{32,0},{64,96},{96,64},{128,160},{160,128},{192,224},{224,1... | collective-permute-start | bytes 208904 | tf_op jit(solution)/shard_map/ppermute | solution.py:322
  85.0 4.5 %collective-permute-start.5 = (f32[136,128]{1,0:T(8,128)S(1)}, f32[136,128]{1,0:T(8,128)S(1)}, u32[]{:S(2)}, u32[]{:S(2)}) collective-permute-start(f32[136,128]{1,0:T(8,128)S(1)} %merge.5.mine_ref), channel_id=1, source_target_pairs={{0,64},{32,96},{64,0},{96,32},{128,192},{160,224},{192,128},{224,1... | collective-permute-start | bytes 208904 | tf_op jit(solution)/shard_map/ppermute | solution.py:322

commit v6 on v5

--- a/solution.py
+++ b/solution.py
@@ -15,7 +15,9 @@
 ROW = ("z", "core")
 COL = ("x", "y")
 TINY = 1e-30
+READY = 7
 LARGE_MIB = 52
+SPLIT_MIB = 60
 WORK_MIB = 12
 
 
@@ -105,14 +107,45 @@
     return jnp.concatenate(strips, axis=0)
 
 
+def split_kernel(t_ref, high_ref, low_ref):
+    high, low = split(t_ref[...])
+    high_ref[...] = high
+    low_ref[...] = low
+
+
+def fetch(t_hbm, high_hbm, low_hbm, t_buf, high_buf, low_buf, sems):
+    ready = high_hbm.shape[0]
+    slices = t_hbm.shape[0]
+    copies = []
+    for k in range(slices):
+        if k < ready:
+            pair = (
+                pltpu.make_async_copy(high_hbm.at[k], high_buf.at[k], sems.at[0, k]),
+                pltpu.make_async_copy(low_hbm.at[k], low_buf.at[k], sems.at[1, k]),
+            )
+        else:
+            pair = (pltpu.make_async_copy(t_hbm.at[k], t_buf.at[k - ready], sems.at[0, k]),)
+        for copy in pair:
+            copy.start()
+        copies.append(pair)
+
+    def halves(k):
+        for copy in copies[k]:
+            copy.wait()
+        if k < ready:
+            return high_buf[k], low_buf[k]
+        return split(t_buf[k - ready])
+
+    return halves
+
+
 def stage_kernel(in_ref, out_ref):
     out_ref[...] = in_ref[...]
 
 
-def first_kernel(own_ref, t_hbm, mine_ref, other_ref, c_ref, out_ref, t_buf, b_block, total, sems):
+def first_kernel(own_ref, t_hbm, high_hbm, low_hbm, mine_ref, other_ref, c_ref, out_ref, b_block, total, t_buf, high_buf, low_buf, sems):
     slices = t_hbm.shape[0]
-    for k in range(slices):
-        pltpu.make_async_copy(t_hbm.at[k], t_buf.at[k], sems.at[k]).start()
+    halves_of = fetch(t_hbm, high_hbm, low_hbm, t_buf, high_buf, low_buf, sems)
     core = own_ref[0]
     b_block[:, core] = mine_ref[...]
     b_block[:, 1 - core] = other_ref[...]
@@ -127,8 +160,7 @@
     for k in range(slices):
         w_high, w_low = split(turned * c_turned[:, k : k + 1])
         w_both = jnp.concatenate([w_high, w_low], axis=0)
-        pltpu.make_async_copy(t_hbm.at[k], t_buf.at[k], sems.at[k]).wait()
-        t_high, t_low = split(t_buf[k])
+        t_high, t_low = halves_of(k)
         main = dot_turned(w_both, t_high)
         rest = dot_turned(w_high, t_low)
         term = main[:width] + (main[width:] + rest)
@@ -181,18 +213,16 @@
     out_ref[width:, :] = jnp.broadcast_to(most, (out_ref.shape[0] - width, width))
 
 
-def second_kernel(own_ref, t_hbm, scaled_ref, c_ref, message_ref, pair_ref, send_ref, keep_ref, total, halves, t_buf, sems):
+def second_kernel(own_ref, t_hbm, high_hbm, low_hbm, scaled_ref, c_ref, message_ref, pair_ref, send_ref, keep_ref, total, halves, t_buf, high_buf, low_buf, sems):
     slices = t_hbm.shape[0]
-    for k in range(slices):
-        pltpu.make_async_copy(t_hbm.at[k], t_buf.at[k], sems.at[k]).start()
+    halves_of = fetch(t_hbm, high_hbm, low_hbm, t_buf, high_buf, low_buf, sems)
     turned = scaled_ref[...].T
     width = turned.shape[0]
     c_turned = c_ref[...].T
     for k in range(slices):
         w_high, w_low = split(turned * c_turned[:, k : k + 1])
         w_both = jnp.concatenate([w_high, w_low], axis=0)
-        pltpu.make_async_copy(t_hbm.at[k], t_buf.at[k], sems.at[k]).wait()
-        t_high, t_low = split(t_buf[k])
+        t_high, t_low = halves_of(k)
         main = jnp.dot(w_both, t_high, preferred_element_type=jnp.float32)
         rest = jnp.dot(w_high, t_low, preferred_element_type=jnp.float32)
         term = main[:width] + (main[width:] + rest)
@@ -261,6 +291,25 @@
     own = jnp.stack([lax.axis_index("core"), lax.axis_index(COL)]).astype(jnp.int32)
     spread_b = jnp.broadcast_to(factor_b[None], (z_size,) + factor_b.shape)
     mine = lax.all_to_all(spread_b, "z", 0, 0, tiled=True)
+    block = (1, rows_block, cols_block)
+    high, low = pl.pallas_call(
+        split_kernel,
+        grid=(READY,),
+        out_shape=(shape((READY,) + block[1:], jnp.bfloat16),) * 2,
+        in_specs=[pl.BlockSpec(block, lambda k: (k, 0, 0))],
+        out_specs=(pl.BlockSpec(block, lambda k: (k, 0, 0)),) * 2,
+        compiler_params=limited(SPLIT_MIB),
+        cost_estimate=pl.CostEstimate(
+            flops=4 * tensor.size, bytes_accessed=8 * tensor.size, transcendentals=0
+        ),
+        name="split",
+    )(tensor)
+    slice_scratch = [
+        pltpu.VMEM((slices - READY,) + block[1:], f32),
+        pltpu.VMEM((READY,) + block[1:], jnp.bfloat16),
+        pltpu.VMEM((READY,) + block[1:], jnp.bfloat16),
+        pltpu.SemaphoreType.DMA((2, slices)),
+    ]
     other = lax.ppermute(mine, "core", swap)
     staged_c = pl.pallas_call(
         stage_kernel,
@@ -273,17 +322,16 @@
     packed = pl.pallas_call(
         first_kernel,
         out_shape=shape((col_size, owned_a + share_a, width), f32),
-        in_specs=[SMEM, HBM, VMEM, VMEM, VMEM],
+        in_specs=[SMEM] + [HBM] * 3 + [VMEM] * 3,
         out_specs=VMEM,
         scratch_shapes=[
-            pltpu.VMEM(tensor.shape, f32),
             pltpu.VMEM((z_size, 2, owned_b, width), f32),
             pltpu.VMEM((width, rows_block), f32),
-            pltpu.SemaphoreType.DMA((slices,)),
-        ],
+        ]
+        + slice_scratch,
         compiler_params=limited(LARGE_MIB),
         name="first",
-    )(own, tensor, mine, other, staged_c)
+    )(own, tensor, high, low, mine, other, staged_c)
     received = lax.all_to_all(packed, COL, 0, 0, tiled=True)
     summed = pl.pallas_call(
         sum_kernel,
@@ -330,20 +378,19 @@
             shape((z_size * owned_b, width), f32),
             shape((z_size, owned_b, width), f32),
         ),
-        in_specs=[SMEM, HBM] + [VMEM] * 4,
+        in_specs=[SMEM] + [HBM] * 3 + [VMEM] * 4,
         out_specs=(VMEM, VMEM),
         scratch_shapes=[
             pltpu.VMEM((width, cols_block), f32),
             pltpu.VMEM((z_size, 2, owned_b, width), f32),
-            pltpu.VMEM(tensor.shape, f32),
-            pltpu.SemaphoreType.DMA((slices,)),
-        ],
+        ]
+        + slice_scratch,
         compiler_params=limited(LARGE_MIB),
         cost_estimate=pl.CostEstimate(
             flops=6 * tensor.size * width, bytes_accessed=4 * tensor.size, transcendentals=0
         ),
         name="second",
-    )(own, tensor, scaled, staged_c, message, pair)
+    )(own, tensor, high, low, scaled, staged_c, message, pair)
     quad = merged(pair, got)
     other_half = lax.ppermute(send, "core", swap)
     got = flipped(quad, 1)

time: 95.8 us -> 104 us (1.086)
  Pallas kernels: 26.2 us -> 34.9 us
    pallas_call x0 -> x1, Pallas kernels: none -> 8.61 us  [per_device(): pl.pallas_call(split_kernel, grid=(READY,), out_shape=(shape((READY,) + b...]
  transfers between devices with their start and end apart: 7 -> 7, of which waited for: 6 -> 5; matrix products, arithmetic and copies ran while one was open for 0% -> 0% of each run, Pallas kernels for 6% -> 14%
where the time goes in v6:
time: 104 us
  blocking collectives  43.2 us (42%)
  Pallas kernels  34.9 us (34%)
  starting transfers between devices  13.7 us (13%)
  waiting for transfers between devices  9.96 us (10%)
  local copies, waits for them, and re-layouts  1.42 us (1%)
    all_to_all x1, blocking collectives, per_device(): mine = lax.all_to_all(spread_b, 'z', 0, 0, tiled=True)  16.6 us
    all_to_all x1, blocking collectives, per_device(): received = lax.all_to_all(packed, COL, 0, 0, tiled=True)  14.9 us
    all_to_all x1, blocking collectives, per_device(): gathered = lax.all_to_all(summed, COL, 0, 0, tiled=True)  11.7 us
    pallas_call x1, Pallas kernels, per_device(): pl.pallas_call(split_kernel, grid=(READY,), out_shape=(shape((READY,) + b...  8.61 us
    ppermute x3, waiting for transfers between devices, flipped(): return lax.ppermute(array, 'z', [(i, i ^ distance) for i in range(z_size)])  8.3 us
    pallas_call x1, Pallas kernels, per_device(): pl.pallas_call(middle_kernel, out_shape=(shape((owned_a, width), f32), sh...  7.42 us
    pallas_call x1, Pallas kernels, per_device(): pl.pallas_call(first_kernel, out_shape=shape((col_size, owned_a + share_a...  6.37 us
    pallas_call x1, Pallas kernels, per_device(): pl.pallas_call(second_kernel, out_shape=(shape((z_size * owned_b, width),...  5.87 us
  transfers between devices with their start and end apart: 7, of which 5 were waited for; matrix products, arithmetic and copies ran while one was open for 0% of the time, Pallas kernels for 14%

profile of v6, /device:TPU:1, one launch (start us, length us, event | category | flops | bytes accessed | tf_op | source)
XLA Modules:
  0.0 103.8 jit_solution(3766984768637488271)
XLA Ops:
  0.6 0.7 broadcast_in_dim.2
  1.4 16.6 %all_to_all.20.mine_ref = f32[8,32,128]{2,1,0:T(8,128)S(1)} all-to-all(f32[8,32,128]{2,1,0:T(8,128)S(1)} %broadcast_in_dim.2), channel_id=1, replica_groups=mesh['z'=8,'core'=2,'x'=4,'y'=4] {'z'}, dimensions={0} | all-to-all | bytes 262144 | tf_op jit(solution)/shard_map/all_to_all | solution.py:293
  17.9 2.3 %collective-permute-start = (f32[8,32,128]{2,1,0:T(8,128)S(1)}, f32[8,32,128]{2,1,0:T(8,128)S(1)}, u32[]{:S(2)}, u32[]{:S(2)}) collective-permute-start(f32[8,32,128]{2,1,0:T(8,128)S(1)} %all_to_all.20.mine_ref), channel_id=1, source_target_pairs={{0,16},{16,0},{1,17},{17,1},{2,18},{18,2},{3,19},{19,3},{4,20},{20... | collective-permute-start | bytes 393224 | tf_op jit(solution)/shard_map/ppermute | solution.py:313
  20.2 0.7 copy-done
  20.9 8.6 %split.1 = (bf16[7,512,512]{2,1,0:T(8,128)(2,1)}, bf16[7,512,512]{2,1,0:T(8,128)(2,1)}) custom-call(f32[12,512,512]{2,1,0:T(8,128)} %t_hbm.3), custom_call_target="tpu_custom_call" | custom-call | flops 12582912 | bytes 25165824 | tf_op jit(solution)/shard_map/split/pallas_call | solution.py:295
  29.6 6.4 %first.1 = f32[16,40,128]{2,1,0:T(8,128)S(1)} custom-call(s32[2]{0:T(128)S(1)} %pad_add_fusion.own_ref, f32[12,512,512]{2,1,0:T(8,128)} %t_hbm.3, bf16[7,512,512]{2,1,0:T(8,128)(2,1)} %get-tuple-element.9.high_hbm, bf16[7,512,512]{2,1,0:T(8,128)(2,1)} %get-tuple-element.10.low_hbm, f32[8,32,128]{2,1,0:T(8,128)S(1)} %all_to_all.20.mine_ref, ...), custom_call_target="tpu_custom_call" | custom-call | tf_op jit(solution)/shard_map/first/pallas_call | solution.py:322
  36.0 14.9 %all_to_all.21.in_ref = f32[16,40,128]{2,1,0:T(8,128)S(1)} all-to-all(f32[16,40,128]{2,1,0:T(8,128)S(1)} %first.1), channel_id=1, replica_groups=mesh['z'=8,'core'=2,'x'=4,'y'=4] {'x','y'}, dimensions={0} | all-to-all | bytes 655360 | tf_op jit(solution)/shard_map/all_to_all | solution.py:335
  50.9 11.7 %all_to_all.22.g_ref = f32[16,40,128]{2,1,0:T(8,128)S(1)} all-to-all(f32[16,40,128]{2,1,0:T(8,128)S(1)} %sum.1), channel_id=1, replica_groups=mesh['z'=8,'core'=2,'x'=4,'y'=4] {'x','y'}, dimensions={0} | all-to-all | bytes 655360 | tf_op jit(solution)/shard_map/all_to_all | solution.py:344
  62.6 7.4 %middle.1 = (f32[32,128]{1,0:T(8,128)}, f32[512,128]{1,0:T(8,128)S(1)}, f32[136,128]{1,0:T(8,128)S(1)}) custom-call(s32[2]{0:T(128)S(1)} %pad_add_fusion.own_ref, f32[16,40,128]{2,1,0:T(8,128)S(1)} %all_to_all.22.g_ref, f32[12,128]{1,0:T(8,128)S(1)} %stage.1.c_ref), custom_call_target="tpu_custom_call" | custom-call | tf_op jit(solution)/shard_map/middle/pallas_call | solution.py:345
  70.1 2.5 %collective-permute-start.1 = (f32[136,128]{1,0:T(8,128)S(1)}, f32[136,128]{1,0:T(8,128)S(1)}, u32[]{:S(2)}, u32[]{:S(2)}) collective-permute-start(f32[136,128]{1,0:T(8,128)S(1)} %get-tuple-element.13.mine_ref.message_ref), channel_id=1, source_target_pairs={{0,16},{16,0},{1,17},{17,1},{2,18},{18,2},{3,19},{19,3},{4,20},{20... | collective-permute-start | bytes 208904 | tf_op jit(solution)/shard_map/ppermute | solution.py:372
  72.6 0.9 collective-permute-done.1.got_ref
  73.5 5.9 %second.1 = (f32[256,128]{1,0:T(8,128)S(1)}, f32[8,32,128]{2,1,0:T(8,128)S(1)}) custom-call(s32[2]{0:T(128)S(1)} %pad_add_fusion.own_ref, f32[12,512,512]{2,1,0:T(8,128)} %t_hbm.3, bf16[7,512,512]{2,1,0:T(8,128)(2,1)} %get-tuple-element.9.high_hbm, bf16[7,512,512]{2,1,0:T(8,128)(2,1)} %get-tuple-element.10.low_hbm, ...), custom_call_target="tpu_custom_call" | custom-call | flops 2415919104 | bytes 12582912 | tf_op jit(solution)/shard_map/second/pallas_call | solution.py:375
  79.4 0.4 collective-permute-start.2
  79.8 0.3 collective-permute-start.3
  80.1 0.7 collective-permute-done.2.got_ref
  80.8 0.7 pair.1
  81.5 5.7 %all-to-all-start.3 = ((f32[8,40,128]{2,1,0:T(8,128)}), f32[8,40,128]{2,1,0:T(8,128)S(1)}, u32[]{:S(2)}, u32[]{:S(2)}) async-start(f32[8,40,128]{2,1,0:T(8,128)} %pair.1), calls=%async_computation.3 | async-start | bytes 327680 | tf_op jit(solution)/shard_map/all_to_all | solution.py:407
  87.2 0.3 collective-permute-done.3.got_ref
  87.5 1.2 %collective-permute-start.4 = (f32[136,128]{1,0:T(8,128)S(1)}, f32[136,128]{1,0:T(8,128)S(1)}, u32[]{:S(2)}, u32[]{:S(2)}) collective-permute-start(f32[136,128]{1,0:T(8,128)S(1)} %merge.4.mine_ref), channel_id=1, source_target_pairs={{0,32},{32,0},{64,96},{96,64},{128,160},{160,128},{192,224},{224,1... | collective-permute-start | bytes 208904 | tf_op jit(solution)/shard_map/ppermute | solution.py:370
  88.7 4.7 %collective-permute-done.4.got_ref = f32[136,128]{1,0:T(8,128)S(1)} collective-permute-done((f32[136,128]{1,0:T(8,128)S(1)}, f32[136,128]{1,0:T(8,128)S(1)}, u32[]{:S(2)}, u32[]{:S(2)}) %collective-permute-start.4) | collective-permute-done | bytes 69664 | tf_op jit(solution)/shard_map/ppermute | solution.py:370
  93.5 1.3 %collective-permute-start.5 = (f32[136,128]{1,0:T(8,128)S(1)}, f32[136,128]{1,0:T(8,128)S(1)}, u32[]{:S(2)}, u32[]{:S(2)}) collective-permute-start(f32[136,128]{1,0:T(8,128)S(1)} %merge.5.mine_ref), channel_id=1, source_target_pairs={{0,64},{32,96},{64,0},{96,32},{128,192},{160,224},{192,128},{224,1... | collective-permute-start | bytes 208904 | tf_op jit(solution)/shard_map/ppermute | solution.py:370
  94.8 3.2 %collective-permute-done.5.got_ref = f32[136,128]{1,0:T(8,128)S(1)} collective-permute-done((f32[136,128]{1,0:T(8,128)S(1)}, f32[136,128]{1,0:T(8,128)S(1)}, u32[]{:S(2)}, u32[]{:S(2)}) %collective-permute-start.5) | collective-permute-done | bytes 69664 | tf_op jit(solution)/shard_map/ppermute | solution.py:370
  98.0 5.0 %solve.1.solved_ref = f32[136,128]{1,0:T(8,128)S(1)} custom-call(f32[136,128]{1,0:T(8,128)S(1)} %merge.5.mine_ref, f32[136,128]{1,0:T(8,128)S(1)} %collective-permute-done.5.got_ref, f32[12,128]{1,0:T(8,128)S(1)} %stage.1.c_ref), custom_call_target="tpu_custom_call" | custom-call | flops 1000000000 | bytes 1000000 | tf_op jit(solution)/shard_map/solve/pallas_call | solution.py:408
  103.0 0.8 last.1
  (9 shorter events, 0.2 us)
Async XLA Ops:
  17.9 11.7 %collective-permute-start = (f32[8,32,128]{2,1,0:T(8,128)S(1)}, f32[8,32,128]{2,1,0:T(8,128)S(1)}, u32[]{:S(2)}, u32[]{:S(2)}) collective-permute-start(f32[8,32,128]{2,1,0:T(8,128)S(1)} %all_to_all.20.mine_ref), channel_id=1, source_target_pairs={{0,16},{16,0},{1,17},{17,1},{2,18},{18,2},{3,19},{19,3},{4,20},{20... | collective-permute-start | bytes 393224 | tf_op jit(solution)/shard_map/ppermute | solution.py:313
  20.2 0.7 copy-start
  70.1 3.4 %collective-permute-start.1 = (f32[136,128]{1,0:T(8,128)S(1)}, f32[136,128]{1,0:T(8,128)S(1)}, u32[]{:S(2)}, u32[]{:S(2)}) collective-permute-start(f32[136,128]{1,0:T(8,128)S(1)} %get-tuple-element.13.mine_ref.message_ref), channel_id=1, source_target_pairs={{0,16},{16,0},{1,17},{17,1},{2,18},{18,2},{3,19},{19,3},{4,20},{20... | collective-permute-start | bytes 208904 | tf_op jit(solution)/shard_map/ppermute | solution.py:372
  79.4 1.4 %collective-permute-start.2 = (f32[256,128]{1,0:T(8,128)S(1)}, f32[256,128]{1,0:T(8,128)S(1)}, u32[]{:S(2)}, u32[]{:S(2)}) collective-permute-start(f32[256,128]{1,0:T(8,128)S(1)} %get-tuple-element.15), channel_id=1, source_target_pairs={{0,16},{16,0},{1,17},{17,1},{2,18},{18,2},{3,19},{19,3},{4,20},{20... | collective-permute-start | bytes 393224 | tf_op jit(solution)/shard_map/ppermute | solution.py:395
  79.8 7.7 %collective-permute-start.3 = (f32[136,128]{1,0:T(8,128)S(1)}, f32[136,128]{1,0:T(8,128)S(1)}, u32[]{:S(2)}, u32[]{:S(2)}) collective-permute-start(f32[136,128]{1,0:T(8,128)S(1)} %merge.3.pair_ref.mine_ref), channel_id=1, source_target_pairs={{0,128},{32,160},{64,192},{96,224},{128,0},{160,32},{192,64},{224,... | collective-permute-start | bytes 208904 | tf_op jit(solution)/shard_map/ppermute | solution.py:370
  81.5 21.5 %all-to-all-start.3 = ((f32[8,40,128]{2,1,0:T(8,128)}), f32[8,40,128]{2,1,0:T(8,128)S(1)}, u32[]{:S(2)}, u32[]{:S(2)}) async-start(f32[8,40,128]{2,1,0:T(8,128)} %pair.1), calls=%async_computation.3 | async-start | bytes 327680 | tf_op jit(solution)/shard_map/all_to_all | solution.py:407
  87.5 6.0 %collective-permute-start.4 = (f32[136,128]{1,0:T(8,128)S(1)}, f32[136,128]{1,0:T(8,128)S(1)}, u32[]{:S(2)}, u32[]{:S(2)}) collective-permute-start(f32[136,128]{1,0:T(8,128)S(1)} %merge.4.mine_ref), channel_id=1, source_target_pairs={{0,32},{32,0},{64,96},{96,64},{128,160},{160,128},{192,224},{224,1... | collective-permute-start | bytes 208904 | tf_op jit(solution)/shard_map/ppermute | solution.py:370
  93.5 4.5 %collective-permute-start.5 = (f32[136,128]{1,0:T(8,128)S(1)}, f32[136,128]{1,0:T(8,128)S(1)}, u32[]{:S(2)}, u32[]{:S(2)}) collective-permute-start(f32[136,128]{1,0:T(8,128)S(1)} %merge.5.mine_ref), channel_id=1, source_target_pairs={{0,64},{32,96},{64,0},{96,32},{128,192},{160,224},{192,128},{224,1... | collective-permute-start | bytes 208904 | tf_op jit(solution)/shard_map/ppermute | solution.py:370

commit v7 on v5

--- a/solution.py
+++ b/solution.py
@@ -15,7 +15,9 @@
 ROW = ("z", "core")
 COL = ("x", "y")
 TINY = 1e-30
+EARLY = 3
 LARGE_MIB = 52
+FIRST_MIB = 46
 WORK_MIB = 12
 
 
@@ -105,14 +107,22 @@
     return jnp.concatenate(strips, axis=0)
 
 
-def stage_kernel(in_ref, out_ref):
-    out_ref[...] = in_ref[...]
-
-
-def first_kernel(own_ref, t_hbm, mine_ref, other_ref, c_ref, out_ref, t_buf, b_block, total, sems):
+def stage_kernel(t_hbm, out_ref, sems):
+    copies = [
+        pltpu.make_async_copy(t_hbm.at[k], out_ref.at[k], sems.at[k])
+        for k in range(out_ref.shape[0])
+    ]
+    for copy in copies:
+        copy.start()
+    for copy in copies:
+        copy.wait()
+
+
+def first_kernel(own_ref, t_hbm, early_ref, mine_ref, other_ref, c_ref, out_ref, t_buf, b_block, total, sems):
     slices = t_hbm.shape[0]
-    for k in range(slices):
-        pltpu.make_async_copy(t_hbm.at[k], t_buf.at[k], sems.at[k]).start()
+    early = early_ref.shape[0]
+    for k in range(early, slices):
+        pltpu.make_async_copy(t_hbm.at[k], t_buf.at[k - early], sems.at[k - early]).start()
     core = own_ref[0]
     b_block[:, core] = mine_ref[...]
     b_block[:, 1 - core] = other_ref[...]
@@ -127,8 +137,11 @@
     for k in range(slices):
         w_high, w_low = split(turned * c_turned[:, k : k + 1])
         w_both = jnp.concatenate([w_high, w_low], axis=0)
-        pltpu.make_async_copy(t_hbm.at[k], t_buf.at[k], sems.at[k]).wait()
-        t_high, t_low = split(t_buf[k])
+        if k < early:
+            t_high, t_low = split(early_ref[k])
+        else:
+            pltpu.make_async_copy(t_hbm.at[k], t_buf.at[k - early], sems.at[k - early]).wait()
+            t_high, t_low = split(t_buf[k - early])
         main = dot_turned(w_both, t_high)
         rest = dot_turned(w_high, t_low)
         term = main[:width] + (main[width:] + rest)
@@ -262,28 +275,32 @@
     spread_b = jnp.broadcast_to(factor_b[None], (z_size,) + factor_b.shape)
     mine = lax.all_to_all(spread_b, "z", 0, 0, tiled=True)
     other = lax.ppermute(mine, "core", swap)
-    staged_c = pl.pallas_call(
+    early = pl.pallas_call(
         stage_kernel,
-        out_shape=pltpu.VMEM(factor_c.shape, f32),
-        in_specs=[VMEM],
-        out_specs=VMEM,
-        compiler_params=small,
+        out_shape=pltpu.VMEM((EARLY, rows_block, cols_block), f32),
+        in_specs=[HBM],
+        out_specs=VMEM,
+        scratch_shapes=[pltpu.SemaphoreType.DMA((EARLY,))],
+        compiler_params=limited(FIRST_MIB),
+        cost_estimate=pl.CostEstimate(
+            flops=0, bytes_accessed=4 * EARLY * rows_block * cols_block, transcendentals=0
+        ),
         name="stage",
-    )(factor_c)
+    )(tensor)
     packed = pl.pallas_call(
         first_kernel,
         out_shape=shape((col_size, owned_a + share_a, width), f32),
-        in_specs=[SMEM, HBM, VMEM, VMEM, VMEM],
+        in_specs=[SMEM, HBM] + [VMEM] * 4,
         out_specs=VMEM,
         scratch_shapes=[
-            pltpu.VMEM(tensor.shape, f32),
+            pltpu.VMEM((slices - EARLY, rows_block, cols_block), f32),
             pltpu.VMEM((z_size, 2, owned_b, width), f32),
             pltpu.VMEM((width, rows_block), f32),
-            pltpu.SemaphoreType.DMA((slices,)),
+            pltpu.SemaphoreType.DMA((slices - EARLY,)),
         ],
-        compiler_params=limited(LARGE_MIB),
+        compiler_params=limited(FIRST_MIB),
         name="first",
-    )(own, tensor, mine, other, staged_c)
+    )(own, tensor, early, mine, other, factor_c)
     received = lax.all_to_all(packed, COL, 0, 0, tiled=True)
     summed = pl.pallas_call(
         sum_kernel,
@@ -306,7 +323,7 @@
         scratch_shapes=[pltpu.VMEM((rows_block, width), f32)],
         compiler_params=limited(WORK_MIB),
         name="middle",
-    )(own, gathered, staged_c)
+    )(own, gathered, factor_c)
 
     def merged(mine, got):
         return pl.pallas_call(
@@ -343,12 +360,12 @@
             flops=6 * tensor.size * width, bytes_accessed=4 * tensor.size, transcendentals=0
         ),
         name="second",
-    )(own, tensor, scaled, staged_c, message, pair)
+    )(own, tensor, scaled, factor_c, message, pair)
     quad = merged(pair, got)
     other_half = lax.ppermute(send, "core", swap)
-    got = flipped(quad, 1)
+    got = flipped(quad, 2)
     octet = merged(quad, got)
-    got = flipped(octet, 2)
+    got = flipped(octet, 1)
     outgoing = pl.pallas_call(
         pair_kernel,
         out_shape=shape((z_size, owned_b + 8, width), f32),
@@ -366,7 +383,7 @@
         compiler_params=small,
         cost_estimate=pl.CostEstimate(flops=10**9, bytes_accessed=10**6, transcendentals=0),
         name="solve",
-    )(octet, got, staged_c)
+    )(octet, got, factor_c)
     b_update = pl.pallas_call(
         last_kernel,
         out_shape=shape((owned_b, width), f32),

time: 95.8 us -> 97.2 us (1.015); the launches traced: 95.3 us -> 95.4 us
    pallas_call x1, Pallas kernels: 0.01 us -> 1.88 us  [per_device(): pl.pallas_call(stage_kernel, out_shape=pltpu.VMEM((EARLY, rows_block, col...]
    pallas_call x1, Pallas kernels: 6.4 us -> 5.36 us  [per_device(): pl.pallas_call(first_kernel, out_shape=shape((col_size, owned_a + share_a...]
  transfers between devices with their start and end apart: 7 -> 7, of which waited for: 6 -> 5; matrix products, arithmetic and copies ran while one was open for 0% -> 0% of each run, Pallas kernels for 6% -> 8%
where the time goes in v7:
time: 97.2 us; the launch traced here: 95.4 us
  blocking collectives  43.2 us (44%)
  Pallas kernels  27 us (28%)
  starting transfers between devices  13.5 us (14%)
  waiting for transfers between devices  10.2 us (10%)
    all_to_all x1, blocking collectives, per_device(): mine = lax.all_to_all(spread_b, 'z', 0, 0, tiled=True)  16.6 us
    all_to_all x1, blocking collectives, per_device(): received = lax.all_to_all(packed, COL, 0, 0, tiled=True)  14.9 us
    all_to_all x1, blocking collectives, per_device(): gathered = lax.all_to_all(summed, COL, 0, 0, tiled=True)  11.7 us
    ppermute x3, waiting for transfers between devices, flipped(): return lax.ppermute(array, 'z', [(i, i ^ distance) for i in range(z_size)])  8.54 us
    pallas_call x1, Pallas kernels, per_device(): pl.pallas_call(middle_kernel, out_shape=(shape((owned_a, width), f32), sh...  7.42 us
    pallas_call x1, Pallas kernels, per_device(): pl.pallas_call(second_kernel, out_shape=(shape((z_size * owned_b, width),...  5.75 us
    all_to_all x1, starting transfers between devices, per_device(): final = lax.all_to_all(outgoing, 'z', 0, 0, tiled=True)  5.66 us
    pallas_call x1, Pallas kernels, per_device(): pl.pallas_call(first_kernel, out_shape=shape((col_size, owned_a + share_a...  5.36 us
  transfers between devices with their start and end apart: 7, of which 5 were waited for; matrix products, arithmetic and copies ran while one was open for 0% of the time, Pallas kernels for 8%

profile of v7, /device:TPU:1, one launch (start us, length us, event | category | flops | bytes accessed | tf_op | source)
XLA Modules:
  0.0 95.4 jit_solution(10537268325407496651)
XLA Ops:
  0.6 0.7 broadcast_in_dim.2
  1.4 16.6 %all_to_all.20.mine_ref = f32[8,32,128]{2,1,0:T(8,128)S(1)} all-to-all(f32[8,32,128]{2,1,0:T(8,128)S(1)} %broadcast_in_dim.2), channel_id=1, replica_groups=mesh['z'=8,'core'=2,'x'=4,'y'=4] {'z'}, dimensions={0} | all-to-all | bytes 262144 | tf_op jit(solution)/shard_map/all_to_all | solution.py:276
  17.9 2.3 %collective-permute-start = (f32[8,32,128]{2,1,0:T(8,128)S(1)}, f32[8,32,128]{2,1,0:T(8,128)S(1)}, u32[]{:S(2)}, u32[]{:S(2)}) collective-permute-start(f32[8,32,128]{2,1,0:T(8,128)S(1)} %all_to_all.20.mine_ref), channel_id=1, source_target_pairs={{0,16},{16,0},{1,17},{17,1},{2,18},{18,2},{3,19},{19,3},{4,20},{20... | collective-permute-start | bytes 393224 | tf_op jit(solution)/shard_map/ppermute | solution.py:277
  20.2 1.9 %stage.1.early_ref = f32[3,512,512]{2,1,0:T(8,128)S(1)} custom-call(f32[12,512,512]{2,1,0:T(8,128)} %t_hbm.5), custom_call_target="tpu_custom_call" | custom-call | bytes 3145728 | tf_op jit(solution)/shard_map/stage/pallas_call | solution.py:278
  22.1 0.1 pad_add_fusion.own_ref
  22.2 5.4 %first.1 = f32[16,40,128]{2,1,0:T(8,128)S(1)} custom-call(s32[2]{0:T(128)S(1)} %pad_add_fusion.own_ref, f32[12,512,512]{2,1,0:T(8,128)} %t_hbm.5, f32[3,512,512]{2,1,0:T(8,128)S(1)} %stage.1.early_ref, f32[8,32,128]{2,1,0:T(8,128)S(1)} %all_to_all.20.mine_ref, f32[8,32,128]{2,1,0:T(8,128)S(1)} %collective-permute-done.other_ref, f32[12,128]{1,0:T(8,128)S(1)} %copy-done), custom_call_target="tpu_custom_call" | custom-call | tf_op jit(solution)/shard_map/first/pallas_call | solution.py:290
  27.6 14.9 %all_to_all.21.in_ref = f32[16,40,128]{2,1,0:T(8,128)S(1)} all-to-all(f32[16,40,128]{2,1,0:T(8,128)S(1)} %first.1), channel_id=1, replica_groups=mesh['z'=8,'core'=2,'x'=4,'y'=4] {'x','y'}, dimensions={0} | all-to-all | bytes 655360 | tf_op jit(solution)/shard_map/all_to_all | solution.py:304
  42.5 11.7 %all_to_all.22.g_ref = f32[16,40,128]{2,1,0:T(8,128)S(1)} all-to-all(f32[16,40,128]{2,1,0:T(8,128)S(1)} %sum.1), channel_id=1, replica_groups=mesh['z'=8,'core'=2,'x'=4,'y'=4] {'x','y'}, dimensions={0} | all-to-all | bytes 655360 | tf_op jit(solution)/shard_map/all_to_all | solution.py:313
  54.2 7.4 %middle.1 = (f32[32,128]{1,0:T(8,128)}, f32[512,128]{1,0:T(8,128)S(1)}, f32[136,128]{1,0:T(8,128)S(1)}) custom-call(s32[2]{0:T(128)S(1)} %pad_add_fusion.own_ref, f32[16,40,128]{2,1,0:T(8,128)S(1)} %all_to_all.22.g_ref, f32[12,128]{1,0:T(8,128)S(1)} %copy-done), custom_call_target="tpu_custom_call" | custom-call | tf_op jit(solution)/shard_map/middle/pallas_call | solution.py:314
  61.6 2.5 %collective-permute-start.1 = (f32[136,128]{1,0:T(8,128)S(1)}, f32[136,128]{1,0:T(8,128)S(1)}, u32[]{:S(2)}, u32[]{:S(2)}) collective-permute-start(f32[136,128]{1,0:T(8,128)S(1)} %get-tuple-element.9.mine_ref.message_ref), channel_id=1, source_target_pairs={{0,16},{16,0},{1,17},{17,1},{2,18},{18,2},{3,19},{19,3},{4,20},{20... | collective-permute-start | bytes 208904 | tf_op jit(solution)/shard_map/ppermute | solution.py:341
  64.2 0.9 collective-permute-done.1.got_ref
  65.1 5.7 %second.1 = (f32[256,128]{1,0:T(8,128)S(1)}, f32[8,32,128]{2,1,0:T(8,128)S(1)}) custom-call(s32[2]{0:T(128)S(1)} %pad_add_fusion.own_ref, f32[12,512,512]{2,1,0:T(8,128)} %t_hbm.5, f32[512,128]{1,0:T(8,128)S(1)} %get-tuple-element.8.scaled_ref, f32[12,128]{1,0:T(8,128)S(1)} %copy-done, f32[136,128]{1,0:T(8,128)S(1)} %get-tuple-element.9.mine_ref.message_ref, ...), custom_call_target="tpu_custom_call" | custom-call | flops 2415919104 | bytes 12582912 | tf_op jit(solution)/shard_map/second/pallas_call | solution.py:344
  70.9 0.4 collective-permute-start.2
  71.3 0.3 collective-permute-start.3
  71.6 0.7 collective-permute-done.2.got_ref
  72.3 0.7 pair.1
  73.0 5.7 %all-to-all-start.3 = ((f32[8,40,128]{2,1,0:T(8,128)}), f32[8,40,128]{2,1,0:T(8,128)S(1)}, u32[]{:S(2)}, u32[]{:S(2)}) async-start(f32[8,40,128]{2,1,0:T(8,128)} %pair.1), calls=%async_computation.3 | async-start | bytes 327680 | tf_op jit(solution)/shard_map/all_to_all | solution.py:377
  78.6 0.3 collective-permute-done.3.got_ref
  79.0 2.1 %collective-permute-start.4 = (f32[136,128]{1,0:T(8,128)S(1)}, f32[136,128]{1,0:T(8,128)S(1)}, u32[]{:S(2)}, u32[]{:S(2)}) collective-permute-start(f32[136,128]{1,0:T(8,128)S(1)} %merge.4.mine_ref), channel_id=1, source_target_pairs={{0,64},{32,96},{64,0},{96,32},{128,192},{160,224},{192,128},{224,1... | collective-permute-start | bytes 208904 | tf_op jit(solution)/shard_map/ppermute | solution.py:339
  81.1 5.1 %collective-permute-done.4.got_ref = f32[136,128]{1,0:T(8,128)S(1)} collective-permute-done((f32[136,128]{1,0:T(8,128)S(1)}, f32[136,128]{1,0:T(8,128)S(1)}, u32[]{:S(2)}, u32[]{:S(2)}) %collective-permute-start.4) | collective-permute-done | bytes 69664 | tf_op jit(solution)/shard_map/ppermute | solution.py:339
  86.2 0.2 collective-permute-start.5
  86.4 3.1 %collective-permute-done.5.got_ref = f32[136,128]{1,0:T(8,128)S(1)} collective-permute-done((f32[136,128]{1,0:T(8,128)S(1)}, f32[136,128]{1,0:T(8,128)S(1)}, u32[]{:S(2)}, u32[]{:S(2)}) %collective-permute-start.5) | collective-permute-done | bytes 69664 | tf_op jit(solution)/shard_map/ppermute | solution.py:339
  89.6 5.0 %solve.1.solved_ref = f32[136,128]{1,0:T(8,128)S(1)} custom-call(f32[136,128]{1,0:T(8,128)S(1)} %merge.5.mine_ref, f32[136,128]{1,0:T(8,128)S(1)} %collective-permute-done.5.got_ref, f32[12,128]{1,0:T(8,128)S(1)} %copy-done), custom_call_target="tpu_custom_call" | custom-call | flops 1000000000 | bytes 1000000 | tf_op jit(solution)/shard_map/solve/pallas_call | solution.py:378
  94.6 0.8 last.1
  (8 shorter events, 0.1 us)
Async XLA Ops:
  0.6 21.6 %copy-start = (f32[12,128]{1,0:T(8,128)S(1)}, f32[12,128]{1,0:T(8,128)}, u32[]{:S(2)}) copy-start(f32[12,128]{1,0:T(8,128)} %c_ref.7) | copy-start | bytes 18436
  17.9 4.3 %collective-permute-start = (f32[8,32,128]{2,1,0:T(8,128)S(1)}, f32[8,32,128]{2,1,0:T(8,128)S(1)}, u32[]{:S(2)}, u32[]{:S(2)}) collective-permute-start(f32[8,32,128]{2,1,0:T(8,128)S(1)} %all_to_all.20.mine_ref), channel_id=1, source_target_pairs={{0,16},{16,0},{1,17},{17,1},{2,18},{18,2},{3,19},{19,3},{4,20},{20... | collective-permute-start | bytes 393224 | tf_op jit(solution)/shard_map/ppermute | solution.py:277
  61.6 3.4 %collective-permute-start.1 = (f32[136,128]{1,0:T(8,128)S(1)}, f32[136,128]{1,0:T(8,128)S(1)}, u32[]{:S(2)}, u32[]{:S(2)}) collective-permute-start(f32[136,128]{1,0:T(8,128)S(1)} %get-tuple-element.9.mine_ref.message_ref), channel_id=1, source_target_pairs={{0,16},{16,0},{1,17},{17,1},{2,18},{18,2},{3,19},{19,3},{4,20},{20... | collective-permute-start | bytes 208904 | tf_op jit(solution)/shard_map/ppermute | solution.py:341
  70.9 1.4 %collective-permute-start.2 = (f32[256,128]{1,0:T(8,128)S(1)}, f32[256,128]{1,0:T(8,128)S(1)}, u32[]{:S(2)}, u32[]{:S(2)}) collective-permute-start(f32[256,128]{1,0:T(8,128)S(1)} %get-tuple-element.11), channel_id=1, source_target_pairs={{0,16},{16,0},{1,17},{17,1},{2,18},{18,2},{3,19},{19,3},{4,20},{20... | collective-permute-start | bytes 393224 | tf_op jit(solution)/shard_map/ppermute | solution.py:365
  71.3 7.7 %collective-permute-start.3 = (f32[136,128]{1,0:T(8,128)S(1)}, f32[136,128]{1,0:T(8,128)S(1)}, u32[]{:S(2)}, u32[]{:S(2)}) collective-permute-start(f32[136,128]{1,0:T(8,128)S(1)} %merge.3.pair_ref.mine_ref), channel_id=1, source_target_pairs={{0,128},{32,160},{64,192},{96,224},{128,0},{160,32},{192,64},{224,... | collective-permute-start | bytes 208904 | tf_op jit(solution)/shard_map/ppermute | solution.py:339
  73.0 21.6 %all-to-all-start.3 = ((f32[8,40,128]{2,1,0:T(8,128)}), f32[8,40,128]{2,1,0:T(8,128)S(1)}, u32[]{:S(2)}, u32[]{:S(2)}) async-start(f32[8,40,128]{2,1,0:T(8,128)} %pair.1), calls=%async_computation.3 | async-start | bytes 327680 | tf_op jit(solution)/shard_map/all_to_all | solution.py:377
  79.0 7.2 %collective-permute-start.4 = (f32[136,128]{1,0:T(8,128)S(1)}, f32[136,128]{1,0:T(8,128)S(1)}, u32[]{:S(2)}, u32[]{:S(2)}) collective-permute-start(f32[136,128]{1,0:T(8,128)S(1)} %merge.4.mine_ref), channel_id=1, source_target_pairs={{0,64},{32,96},{64,0},{96,32},{128,192},{160,224},{192,128},{224,1... | collective-permute-start | bytes 208904 | tf_op jit(solution)/shard_map/ppermute | solution.py:339
  86.2 3.4 %collective-permute-start.5 = (f32[136,128]{1,0:T(8,128)S(1)}, f32[136,128]{1,0:T(8,128)S(1)}, u32[]{:S(2)}, u32[]{:S(2)}) collective-permute-start(f32[136,128]{1,0:T(8,128)S(1)} %merge.5.mine_ref), channel_id=1, source_target_pairs={{0,32},{32,0},{64,96},{96,64},{128,160},{160,128},{192,224},{224,1... | collective-permute-start | bytes 208904 | tf_op jit(solution)/shard_map/ppermute | solution.py:339
